TPU v7x, 512 devices: a whole 4x8x8 slice. The times are simulated.
512 devices in a mesh: wide: 64 (over x, y, core), narrow: 8 (over z).
Axes of the slice: x: 4, y: 8, z: 8, core: 2. Of those that a mesh axis runs over, the one named last changes fastest.
Arguments:
- solution: float32 [640, 320, 320], P('wide', 'narrow'), may hold values from -6 to 6
- residual: float32 [640, 320, 320], P('wide', 'narrow'), may hold values from -45 to 45
- direction: float32 [640, 320, 320], P('wide', 'narrow'), may hold values from -14 to 14
- previous_product: float32 [1], replicated, may hold values from 9830400 to 98304000
- basis_x: float32 [640, 640], P('wide'), may hold values from -0.25 to 0.25
- basis_y: float32 [320, 320], P('narrow'), may hold values from -0.3125 to 0.3125
- basis_z: float32 [320, 320], P('narrow'), may hold values from -0.3125 to 0.3125
- eigen_x: float32 [640], replicated, may hold values from 0.2 to 4
- eigen_y: float32 [320], replicated, may hold values from 0.2 to 4
- eigen_z: float32 [320], replicated, may hold values from 0.2 to 4
Outputs:
- solution: float32 [640, 320, 320], P('wide', 'narrow')
- residual: float32 [640, 320, 320], P('wide', 'narrow')
- direction: float32 [640, 320, 320], P('wide', 'narrow')
All inputs are finite; a program needn't handle non-finite values.
Results may differ from a plain program's by a relative error of at most 0.00021.
Values sent between devices are 32-bit elements; how exact they have to be, the bound alone decides.
A program may use at most 64 MiB of HBM per device.

v0:
```python
import functools

import jax
import jax.numpy as jnp
from jax import lax
from jax.sharding import Mesh
from jax.sharding import PartitionSpec as P

WIDE = ("wide_0", "wide_1", "wide_2")
WIDE_NARROW = ("wide_0", "wide_1", "wide_2", "narrow")


mass_band = (
    1.0 / 5040.0,
    1.0 / 42.0,
    397.0 / 1680.0,
    151.0 / 315.0,
    397.0 / 1680.0,
    1.0 / 42.0,
    1.0 / 5040.0,
)
stiff_band = (-1.0 / 120.0, -0.2, -0.125, 2.0 / 3.0, -0.125, -0.2, -1.0 / 120.0)
highest = lax.Precision.HIGHEST


def side_by_side(arrays, axis, dim, along):
    both = jnp.concatenate(arrays, axis=along)
    whole, at, gathered = (lax.all_gather(both, axis, axis=dim, tiled=True), 0, [])
    for a in arrays:
        gathered.append(lax.slice_in_dim(whole, at, at + a.shape[along], axis=along))
        at += a.shape[along]
    return tuple(gathered)


def padded_2(x, sides, width):
    for axis, dim in sides:
        count, length = (lax.axis_size(axis), x.shape[dim])
        up = [(i, (i + 1) % count) for i in range(count - 1)]
        down = [(j, i) for i, j in up]
        last = lax.slice_in_dim(x, length - width, length, axis=dim)
        leading = lax.slice_in_dim(x, 0, width, axis=dim)
        before = lax.ppermute(last, axis, up)
        after = lax.ppermute(leading, axis, down)
        x = jnp.concatenate([before, x, after], axis=dim)
    return x


def in_blocks(x, dim, count):
    before, after = (x.shape[:dim], x.shape[dim + 1 :])
    return jnp.moveaxis(x.reshape(*before, count, -1, *after), dim, 0)


def in_order(parts, dim):
    parts = jnp.moveaxis(parts, 0, dim)
    shape = parts.shape
    return parts.reshape(*shape[:dim], shape[dim] * shape[dim + 1], *shape[dim + 2 :])


def exchange_in_order(parts, axes, turns):
    inside = parts.shape[1:]
    whole = parts.reshape(*(lax.axis_size(a) for a in axes), *inside)
    for k in turns:
        whole = lax.all_to_all(whole, axes[k], k, k, tiled=True)
    return whole.reshape(-1, *inside)


def two_step_exchange(x, groups, turns, split_dim, concat_dim):
    count = lax.axis_size(groups[0]) * lax.axis_size(groups[1])
    parts = in_blocks(x, split_dim, count)
    return in_order(exchange_in_order(parts, groups, turns), concat_dim)


def one_axis_at_a_time(x, axes):
    return functools.reduce(lax.psum, axes, x)


def banded(field, coeffs, axis, length):
    total = coeffs[0] * lax.slice_in_dim(field, 0, length, axis=axis)
    for offset in range(1, 7):
        total = total + coeffs[offset] * lax.slice_in_dim(field, offset, offset + length, axis=axis)
    return total


def apply_padded(padded, length_x, length_y):
    length_z = padded.shape[2]
    along_z = jnp.pad(padded, ((0, 0), (0, 0), (3, 3)))
    mass_z = banded(along_z, mass_band, 2, length_z)
    stiff_z = banded(along_z, stiff_band, 2, length_z)
    first = banded(mass_z, mass_band, 1, length_y)
    second = banded(mass_z, stiff_band, 1, length_y) + banded(stiff_z, mass_band, 1, length_y)
    return banded(first, stiff_band, 0, length_x) + banded(second, mass_band, 0, length_x)


def contract_first(left, right):
    return lax.dot_general(left, right, (((0,), (0,)), ((), ())), precision=highest)


def contract_last(left, right):
    return lax.dot_general(left, right, (((1,), (1,)), ((), ())), precision=highest)


def per_device(
    solution,
    residual,
    direction,
    previous_product,
    basis_x,
    basis_y,
    basis_z,
    eigen_x,
    eigen_y,
    eigen_z,
):
    whole_x = lax.all_gather(basis_x, WIDE, axis=0, tiled=True)
    whole_y, whole_z = side_by_side((basis_y, basis_z), "narrow", 0, 1)
    count_wide = lax.axis_size(WIDE)
    count_narrow = lax.axis_size("narrow")
    index_wide = lax.axis_index(WIDE)
    index_narrow = lax.axis_index("narrow")
    cells_x, cells_y, cells_z = residual.shape
    total_x = whole_x.shape[0]
    total_y = whole_y.shape[0]

    def image_of(field):
        padded = padded_2(field, ((WIDE, 0), ("narrow", 1)), 3)
        return apply_padded(padded, cells_x, cells_y)

    product_before = previous_product[0]
    image = image_of(direction)
    curvature = jnp.sum(direction * image)
    spectral = jnp.dot(residual.reshape(cells_x * cells_y, cells_z), whole_z, precision=highest)
    flat = jnp.transpose(spectral.reshape(cells_x, cells_y, cells_z), (1, 2, 0)).reshape(
        cells_y, cells_z * cells_x
    )
    pencil = contract_first(
        whole_y, lax.all_to_all(flat, "narrow", split_axis=1, concat_axis=0, tiled=True)
    )
    rows_y = total_y // count_wide
    part_z = cells_z // count_narrow
    moved = two_step_exchange(pencil, (("wide_0", "wide_1"), "wide_2"), (1, 0), 0, 1)
    lined = jnp.transpose(moved.reshape(rows_y, count_wide, part_z, cells_x), (0, 2, 1, 3))
    lined = lined.reshape(rows_y * part_z, total_x)
    spectral_x = jnp.dot(lined, whole_x, precision=highest)
    shift_y = lax.dynamic_slice_in_dim(eigen_y, index_wide * rows_y, rows_y)
    shift_z = lax.dynamic_slice_in_dim(eigen_z, index_narrow * part_z, part_z)
    shift_yz = (shift_y[:, None] + shift_z[None, :]).reshape(rows_y * part_z, 1)
    scaled = spectral_x / (eigen_x[None, :] + shift_yz)
    inverse_x = contract_last(scaled, whole_x)
    unlined = jnp.transpose(inverse_x.reshape(rows_y, part_z, count_wide, cells_x), (0, 2, 1, 3))
    unlined = unlined.reshape(rows_y, count_wide * part_z * cells_x)
    pencil = lax.all_to_all(unlined, WIDE, split_axis=1, concat_axis=0, tiled=True)
    pencil = jnp.dot(whole_y, pencil, precision=highest)
    back = lax.all_to_all(pencil, "narrow", split_axis=0, concat_axis=1, tiled=True)
    brick = jnp.transpose(back.reshape(cells_y, cells_z, cells_x), (2, 0, 1))
    result = contract_last(brick.reshape(cells_x * cells_y, cells_z), whole_z)
    precond = result.reshape(cells_x, cells_y, cells_z)
    fresh = image_of(precond)
    items = (jnp.sum(residual * precond), jnp.sum(precond * fresh), jnp.sum(precond * image))
    merged_items = items + (curvature,)
    product_now, self_term, cross_term, curvature = jax.tree.map(
        lambda part: one_axis_at_a_time(part, WIDE_NARROW), merged_items
    )
    ratio = product_now / product_before
    curvature = self_term + 2.0 * ratio * cross_term + ratio * ratio * curvature
    alpha = product_now / curvature
    direction = precond + ratio * direction
    image = fresh + ratio * image
    solution = solution + alpha * direction
    residual = residual - alpha * image
    return (solution, residual, direction)


def solution(mesh):
    torus = Mesh(
        mesh.devices.reshape(4, 8, 2, mesh.shape["narrow"]),
        ("wide_0", "wide_1", "wide_2", "narrow"),
    )
    in_specs = (
        P(WIDE, "narrow", None),
        P(WIDE, "narrow", None),
        P(WIDE, "narrow", None),
        P(),
        P(WIDE, None),
        P("narrow", None),
        P("narrow", None),
        P(),
        P(),
        P(),
    )
    out_specs = (P(WIDE, "narrow", None), P(WIDE, "narrow", None), P(WIDE, "narrow", None))
    return jax.shard_map(
        per_device, mesh=torus, in_specs=in_specs, out_specs=out_specs, check_vma=False
    )
```

profile of v0, /device:TPU:1, one launch (start us, length us, event | category | flops | bytes accessed | tf_op | source)
XLA Modules:
  0.0 284.1 jit_solution(6814553588277534287)
XLA Ops:
  7.9 0.9 pad_maximum_fusion.2
  8.9 28.4 %all_gather.6 = f32[320,640]{1,0:T(8,128)S(1)} all-gather(f32[40,640]{1,0:T(8,128)S(1)} %pad_maximum_fusion.2), channel_id=1, replica_groups=mesh['wide_0'=4,'wide_1'=8,'wide_2'=2,'narrow'=8] {'narrow'}, dimensions={0}, use_global_device_ids=true | all-gather | bytes 921600 | tf_op jit(solution)/shard_map/all_gather | solution.py:28
  37.3 2.3 fusion.46
  39.5 3.5 %copy.43 = f32[10,40,320]{1,0,2:T(8,128)S(1)} copy(f32[10,40,320]{2,1,0:T(8,128)} %bitcast.68) | data formatting | bytes 1024000 | tf_op jit(solution)/shard_map/reshape | solution.py:132
  43.0 1.3 all_to_all.44
  44.3 2.9 %copy.44 = f32[40,8,400]{2,0,1:T(8,128)} copy(f32[40,8,400]{0,2,1:T(8,128)} %all_to_all.44) | data formatting | bytes 1024000 | tf_op jit(solution)/shard_map/all_to_all | solution.py:136
  47.2 3.5 %all-to-all-start = ((f32[40,8,400]{2,0,1:T(8,128)}), f32[40,8,400]{2,0,1:T(8,128)S(1)}, u32[]{:S(2)}, u32[]{:S(2)}) async-start(f32[40,8,400]{2,0,1:T(8,128)} %copy.44), calls=%async_computation | async-start | bytes 1310720 | tf_op jit(solution)/shard_map/all_to_all | solution.py:136
  50.8 0.8 slice_bitcast_fusion
  51.9 12.6 %all-to-all-done = f32[40,8,400]{2,0,1:T(8,128)S(1)} async-done(((f32[40,8,400]{2,0,1:T(8,128)}), f32[40,8,400]{2,0,1:T(8,128)S(1)}, u32[]{:S(2)}, u32[]{:S(2)}) %all-to-all-start) | async-done | bytes 512032 | tf_op jit(solution)/shard_map/all_to_all | solution.py:136
  64.5 1.3 fusion.42
  65.8 11.5 %all_to_all.61 = f32[32,2,5,400]{3,0,2,1:T(8,128)S(1)} all-to-all(f32[32,2,5,400]{3,0,2,1:T(8,128)S(1)} %fusion.42), channel_id=1, replica_groups=mesh['wide_0'=4,'wide_1'=8,'wide_2'=2,'narrow'=8] {'wide_2'}, dimensions={1} | all-to-all | bytes 1024000 | tf_op jit(solution)/shard_map/all_to_all | solution.py:63
  77.2 1.3 copy.47
  78.6 9.9 %all-to-all-start.2 = ((f32[32,2,5,400]{3,1,2,0:T(2,128)}), f32[32,2,5,400]{3,1,2,0:T(2,128)S(1)}, u32[]{:S(2)}, u32[]{:S(2)}) async-start(f32[32,2,5,400]{3,1,2,0:T(2,128)} %copy.47), calls=%async_computation.2 | async-start | bytes 1310720 | tf_op jit(solution)/shard_map/all_to_all | solution.py:63
  88.5 0.8 dynamic_slice.7
  89.2 0.8 dynamic_slice.6
  90.1 15.9 %all-to-all-done.2 = f32[32,2,5,400]{3,1,2,0:T(2,128)S(1)} async-done(((f32[32,2,5,400]{3,1,2,0:T(2,128)}), f32[32,2,5,400]{3,1,2,0:T(2,128)S(1)}, u32[]{:S(2)}, u32[]{:S(2)}) %all-to-all-start.2) | async-done | bytes 512032 | tf_op jit(solution)/shard_map/all_to_all | solution.py:63
  107.1 1.3 reshape_reshape.4
  108.4 4.6 %copy.50 = f32[5,40,64,10]{1,0,3,2:T(8,128)S(1)} copy(f32[5,40,64,10]{2,3,1,0:T(8,128)} %bitcast.62) | data formatting | bytes 1024000 | tf_op jit(solution)/shard_map/transpose | solution.py:141
  113.5 1.9 reshape.75
  115.4 1.7 convolution_divide_fusion
  117.1 1.7 fusion.53
  119.4 2.8 copy.52
  122.3 1.5 all_to_all.50
  123.7 0.9 copy.53
  124.6 1.9 reshape.78
  126.6 9.4 %all-to-all-start.3 = ((f32[64,1,2000]{2,1,0:T(1,128)}), f32[64,1,2000]{2,1,0:T(1,128)S(1)}, u32[]{:S(2)}, u32[]{:S(2)}) async-start(f32[64,1,2000]{2,1,0:T(1,128)} %reshape.78), calls=%async_computation.3 | async-start | bytes 1048576 | tf_op jit(solution)/shard_map/all_to_all | solution.py:151
  136.0 3.5 %collective-permute-start.4 = (f32[3,40,320]{2,1,0:T(8,128)S(1)}, f32[3,40,320]{2,1,0:T(8,128)S(1)}, u32[]{:S(2)}, u32[]{:S(2)}) collective-permute-start(f32[3,40,320]{2,1,0:T(8,128)S(1)} %get-tuple-element.38), channel_id=1, source_target_pairs={{0,8},{8,16},{16,24},{24,32},{32,40},{40,48},{48,56},{56,64},{64,7... | collective-permute-start | bytes 460808 | tf_op jit(solution)/shard_map/ppermute | solution.py:42
  139.6 2.1 collective-permute-start.5
  141.7 7.5 %collective-permute-done.4 = f32[3,40,320]{2,1,0:T(8,128)S(1)} collective-permute-done((f32[3,40,320]{2,1,0:T(8,128)S(1)}, f32[3,40,320]{2,1,0:T(8,128)S(1)}, u32[]{:S(2)}, u32[]{:S(2)}) %collective-permute-start.4) | collective-permute-done | bytes 153632 | tf_op jit(solution)/shard_map/ppermute | solution.py:42
  149.2 0.7 constant_dynamic-update-slice_fusion.2
  149.9 0.9 constant_dynamic-update-slice_fusion.1
  150.8 2.8 all-to-all-done.3
  154.1 1.9 reduce
  156.9 0.9 copy-done.5
  157.8 2.1 fusion.14
  159.8 4.2 %all-to-all-start.4 = ((f32[8,40,400]{2,1,0:T(8,128)}), f32[8,40,400]{2,1,0:T(8,128)}, u32[]{:S(2)}, u32[]{:S(2)}) async-start(f32[8,40,400]{2,1,0:T(8,128)} %fusion.14), calls=%async_computation.4 | async-start | bytes 1310720 | tf_op jit(solution)/shard_map/all_to_all | solution.py:153
  164.0 0.7 constant_dynamic-update-slice_fusion
  164.7 1.1 fusion.50
  165.8 1.3 collective-permute-start.7
  167.1 4.0 %collective-permute-start.6 = (f32[16,3,320]{2,1,0:T(4,128)S(1)}, f32[16,3,320]{2,1,0:T(4,128)S(1)}, u32[]{:S(2)}, u32[]{:S(2)}) collective-permute-start(f32[16,3,320]{2,1,0:T(4,128)S(1)} %get-tuple-element.31), channel_id=1, source_target_pairs={{0,1},{1,2},{2,3},{3,4},{4,5},{5,6},{6,7},{8,9},{9,10},{10,11},{11... | collective-permute-start | bytes 184328 | tf_op jit(solution)/shard_map/ppermute | solution.py:42
  171.7 8.4 %collective-permute-done.7 = f32[16,3,320]{2,1,0:T(4,128)S(1)} collective-permute-done((f32[16,3,320]{2,1,0:T(4,128)S(1)}, f32[16,3,320]{2,1,0:T(4,128)S(1)}, u32[]{:S(2)}, u32[]{:S(2)}) %collective-permute-start.7) | collective-permute-done | bytes 61472 | tf_op jit(solution)/shard_map/ppermute | solution.py:43
  180.2 1.3 pad_maximum_fusion.1
  181.5 3.8 %multiply_add_fusion.1 = (f32[16,46,320]{2,1,0:T(8,128)S(1)}, f32[16,46,320]{2,1,0:T(8,128)S(1)}) fusion(f32[16,46,320]{2,1,0:T(8,128)S(1)} %pad_maximum_fusion.1), kind=kLoop, calls=%fused_computation.4 | loop fusion | flops 6123520 | bytes 2826240 | tf_op jit(solution)/shard_map/add | solution.py:80
  185.3 2.8 copy.55
  188.1 2.7 reshape.71
  190.9 2.9 %copy.56 = f32[10,40,320]{2,1,0:T(8,128)} copy(f32[10,40,320]{1,0,2:T(8,128)} %bitcast.61) | data formatting | bytes 1024000 | tf_op jit(solution)/shard_map/transpose | solution.py:154
  193.8 2.6 fusion.44
  196.4 5.1 %collective-permute-start.1 = (f32[3,40,320]{2,1,0:T(8,128)S(1)}, f32[3,40,320]{2,1,0:T(8,128)S(1)}, u32[]{:S(2)}, u32[]{:S(2)}) collective-permute-start(f32[3,40,320]{2,1,0:T(8,128)S(1)} %bitcast.71), channel_id=1, source_target_pairs={{8,0},{16,8},{24,16},{32,24},{40,32},{48,40},{56,48},{64,56},{72,6... | collective-permute-start | bytes 460808 | tf_op jit(solution)/shard_map/ppermute | solution.py:43
  201.5 2.1 collective-permute-start
  203.7 1.6 fusion.1
  205.3 0.8 collective-permute-done
  206.2 1.3 collective-permute-start.3
  207.5 4.3 %collective-permute-start.2 = (f32[16,3,320]{2,1,0:T(4,128)S(1)}, f32[16,3,320]{2,1,0:T(4,128)S(1)}, u32[]{:S(2)}, u32[]{:S(2)}) collective-permute-start(f32[16,3,320]{2,1,0:T(4,128)S(1)} %get-tuple-element.33), channel_id=1, source_target_pairs={{0,1},{1,2},{2,3},{3,4},{4,5},{5,6},{6,7},{8,9},{9,10},{10,11},{11... | collective-permute-start | bytes 184328 | tf_op jit(solution)/shard_map/ppermute | solution.py:42
  211.7 0.8 multiply_add_fusion.4
  212.8 1.0 collective-permute-done.2
  214.0 3.8 %multiply_add_fusion.3 = (f32[16,46,320]{2,1,0:T(8,128)S(1)}, f32[16,46,320]{2,1,0:T(8,128)S(1)}) fusion(f32[16,46,320]{2,1,0:T(8,128)S(1)} %pad_maximum_fusion), kind=kLoop, calls=%fused_computation.6 | loop fusion | flops 6123520 | bytes 2826240 | tf_op jit(solution)/shard_map/add | solution.py:80
  217.8 0.8 multiply_add_fusion.5
  218.6 1.6 fusion.8
  220.3 2.3 multiply_reduce_fusion
  222.6 8.3 %all-reduce.4 = (f32[]{:T(128)}, f32[]{:T(128)}, f32[]{:T(128)}, f32[]{:T(128)}) all-reduce(f32[]{:T(128)} %get-tuple-element.6, f32[]{:T(128)} %get-tuple-element.5, f32[]{:T(128)} %get-tuple-element.4, f32[]{:T(128)} %get-tuple-element.3), channel_id=1, replica_groups=mesh['wide_0'=4,'wide_1'=8,'wide_2'=2,'narrow'=8] {'wide_0'}, use_global_device_ids=true, to_apply=%region_1.2 | all-reduce | flops 4 | bytes 32 | tf_op jit(solution)/shard_map/psum | solution.py:74
  230.9 14.1 %all-reduce.3 = (f32[]{:T(128)}, f32[]{:T(128)}, f32[]{:T(128)}, f32[]{:T(128)}) all-reduce(f32[]{:T(128)} %get-tuple-element.15, f32[]{:T(128)} %get-tuple-element.16, f32[]{:T(128)} %get-tuple-element.17, f32[]{:T(128)} %get-tuple-element.18), channel_id=1, replica_groups=mesh['wide_0'=4,'wide_1'=8,'wide_2'=2,'narrow'=8] {'wide_1'}, use_global_device_ids=true, to_apply=%region_2.3 | all-reduce | flops 4 | bytes 32 | tf_op jit(solution)/shard_map/psum | solution.py:74
  245.1 11.2 %all-reduce.5 = (f32[]{:T(128)}, f32[]{:T(128)}, f32[]{:T(128)}, f32[]{:T(128)}) all-reduce(f32[]{:T(128)} %get-tuple-element.11, f32[]{:T(128)} %get-tuple-element.12, f32[]{:T(128)} %get-tuple-element.13, f32[]{:T(128)} %get-tuple-element.14), channel_id=1, replica_groups=mesh['wide_0'=4,'wide_1'=8,'wide_2'=2,'narrow'=8] {'wide_2'}, use_global_device_ids=true, to_apply=%region_3.4 | all-reduce | flops 4 | bytes 32 | tf_op jit(solution)/shard_map/psum | solution.py:74
  256.2 15.6 %all-reduce.2 = (f32[]{:T(128)}, f32[]{:T(128)}, f32[]{:T(128)}, f32[]{:T(128)}) all-reduce(f32[]{:T(128)} %get-tuple-element.19, f32[]{:T(128)} %get-tuple-element.20, f32[]{:T(128)} %get-tuple-element.21, f32[]{:T(128)} %get-tuple-element.22), channel_id=1, replica_groups=mesh['wide_0'=4,'wide_1'=8,'wide_2'=2,'narrow'=8] {'narrow'}, use_global_device_ids=true, to_apply=%region_4.5 | all-reduce | flops 4 | bytes 32 | tf_op jit(solution)/shard_map/psum | solution.py:74
  274.9 2.4 multiply_add_fusion.6
  (38 shorter events, 5.1 us)
Async XLA Ops:
  7.2 30.1 %copy-start.3 = (f32[10,40,320]{2,1,0:T(8,128)S(1)}, f32[10,40,320]{2,1,0:T(8,128)}, u32[]{:S(2)}) copy-start(f32[10,40,320]{2,1,0:T(8,128)} %param.11) | copy-start | bytes 1536004
  7.2 106.3 %all-gather.3.cloned.1.call-start = ((), (), s32[]{:S(2)}) async-start(), calls=%async_computation.5 | async-start | bytes 2662400 | tf_op jit(solution)/shard_map/all_gather | solution.py:114
  37.3 13.5 %copy-start.2 = (f32[320,640]{1,0:T(8,128)}, f32[320,640]{1,0:T(8,128)S(1)}, u32[]{:S(2)}) copy-start(f32[320,640]{1,0:T(8,128)S(1)} %all_gather.6) | copy-start | bytes 2457604
  47.2 17.3 %all-to-all-start = ((f32[40,8,400]{2,0,1:T(8,128)}), f32[40,8,400]{2,0,1:T(8,128)S(1)}, u32[]{:S(2)}, u32[]{:S(2)}) async-start(f32[40,8,400]{2,0,1:T(8,128)} %copy.44), calls=%async_computation | async-start | bytes 1310720 | tf_op jit(solution)/shard_map/all_to_all | solution.py:136
  78.6 27.5 %all-to-all-start.2 = ((f32[32,2,5,400]{3,1,2,0:T(2,128)}), f32[32,2,5,400]{3,1,2,0:T(2,128)S(1)}, u32[]{:S(2)}, u32[]{:S(2)}) async-start(f32[32,2,5,400]{3,1,2,0:T(2,128)} %copy.47), calls=%async_computation.2 | async-start | bytes 1310720 | tf_op jit(solution)/shard_map/all_to_all | solution.py:63
  113.5 1.9 copy-start.6
  124.6 11.4 %copy-start = (f32[10,40,320]{2,1,0:T(8,128)S(1)}, f32[10,40,320]{2,1,0:T(8,128)}, u32[]{:S(2)}) copy-start(f32[10,40,320]{2,1,0:T(8,128)} %param.12) | copy-start | bytes 1536004
  126.6 27.0 %all-to-all-start.3 = ((f32[64,1,2000]{2,1,0:T(1,128)}), f32[64,1,2000]{2,1,0:T(1,128)S(1)}, u32[]{:S(2)}, u32[]{:S(2)}) async-start(f32[64,1,2000]{2,1,0:T(1,128)} %reshape.78), calls=%async_computation.3 | async-start | bytes 1048576 | tf_op jit(solution)/shard_map/all_to_all | solution.py:151
  136.0 13.2 %collective-permute-start.4 = (f32[3,40,320]{2,1,0:T(8,128)S(1)}, f32[3,40,320]{2,1,0:T(8,128)S(1)}, u32[]{:S(2)}, u32[]{:S(2)}) collective-permute-start(f32[3,40,320]{2,1,0:T(8,128)S(1)} %get-tuple-element.38), channel_id=1, source_target_pairs={{0,8},{8,16},{16,24},{24,32},{32,40},{40,48},{48,56},{56,64},{64,7... | collective-permute-start | bytes 460808 | tf_op jit(solution)/shard_map/ppermute | solution.py:42
  139.6 24.4 %collective-permute-start.5 = (f32[3,40,320]{2,1,0:T(8,128)S(1)}, f32[3,40,320]{2,1,0:T(8,128)S(1)}, u32[]{:S(2)}, u32[]{:S(2)}) collective-permute-start(f32[3,40,320]{2,1,0:T(8,128)S(1)} %get-tuple-element.37), channel_id=1, source_target_pairs={{8,0},{16,8},{24,16},{32,24},{40,32},{48,40},{56,48},{64,56},{72,6... | collective-permute-start | bytes 460808 | tf_op jit(solution)/shard_map/ppermute | solution.py:43
  156.7 1.0 copy-start.5
  159.8 25.5 %all-to-all-start.4 = ((f32[8,40,400]{2,1,0:T(8,128)}), f32[8,40,400]{2,1,0:T(8,128)}, u32[]{:S(2)}, u32[]{:S(2)}) async-start(f32[8,40,400]{2,1,0:T(8,128)} %fusion.14), calls=%async_computation.4 | async-start | bytes 1310720 | tf_op jit(solution)/shard_map/all_to_all | solution.py:153
  165.8 14.4 %collective-permute-start.7 = (f32[16,3,320]{2,1,0:T(4,128)S(1)}, f32[16,3,320]{2,1,0:T(4,128)S(1)}, u32[]{:S(2)}, u32[]{:S(2)}) collective-permute-start(f32[16,3,320]{2,1,0:T(4,128)S(1)} %get-tuple-element.32), channel_id=1, source_target_pairs={{1,0},{2,1},{3,2},{4,3},{5,4},{6,5},{7,6},{9,8},{10,9},{11,10},{12... | collective-permute-start | bytes 184328 | tf_op jit(solution)/shard_map/ppermute | solution.py:43
  167.1 13.1 %collective-permute-start.6 = (f32[16,3,320]{2,1,0:T(4,128)S(1)}, f32[16,3,320]{2,1,0:T(4,128)S(1)}, u32[]{:S(2)}, u32[]{:S(2)}) collective-permute-start(f32[16,3,320]{2,1,0:T(4,128)S(1)} %get-tuple-element.31), channel_id=1, source_target_pairs={{0,1},{1,2},{2,3},{3,4},{4,5},{5,6},{6,7},{8,9},{9,10},{10,11},{11... | collective-permute-start | bytes 184328 | tf_op jit(solution)/shard_map/ppermute | solution.py:42
  196.4 8.9 %collective-permute-start.1 = (f32[3,40,320]{2,1,0:T(8,128)S(1)}, f32[3,40,320]{2,1,0:T(8,128)S(1)}, u32[]{:S(2)}, u32[]{:S(2)}) collective-permute-start(f32[3,40,320]{2,1,0:T(8,128)S(1)} %bitcast.71), channel_id=1, source_target_pairs={{8,0},{16,8},{24,16},{32,24},{40,32},{48,40},{56,48},{64,56},{72,6... | collective-permute-start | bytes 460808 | tf_op jit(solution)/shard_map/ppermute | solution.py:43
  201.5 4.6 %collective-permute-start = (f32[3,40,320]{2,1,0:T(8,128)S(1)}, f32[3,40,320]{2,1,0:T(8,128)S(1)}, u32[]{:S(2)}, u32[]{:S(2)}) collective-permute-start(f32[3,40,320]{2,1,0:T(8,128)S(1)} %bitcast.70), channel_id=1, source_target_pairs={{0,8},{8,16},{16,24},{24,32},{32,40},{40,48},{48,56},{56,64},{64,7... | collective-permute-start | bytes 460808 | tf_op jit(solution)/shard_map/ppermute | solution.py:42
  206.2 6.6 %collective-permute-start.3 = (f32[16,3,320]{2,1,0:T(4,128)S(1)}, f32[16,3,320]{2,1,0:T(4,128)S(1)}, u32[]{:S(2)}, u32[]{:S(2)}) collective-permute-start(f32[16,3,320]{2,1,0:T(4,128)S(1)} %get-tuple-element.34), channel_id=1, source_target_pairs={{1,0},{2,1},{3,2},{4,3},{5,4},{6,5},{7,6},{9,8},{10,9},{11,10},{12... | collective-permute-start | bytes 184328 | tf_op jit(solution)/shard_map/ppermute | solution.py:43
  207.5 6.3 %collective-permute-start.2 = (f32[16,3,320]{2,1,0:T(4,128)S(1)}, f32[16,3,320]{2,1,0:T(4,128)S(1)}, u32[]{:S(2)}, u32[]{:S(2)}) collective-permute-start(f32[16,3,320]{2,1,0:T(4,128)S(1)} %get-tuple-element.33), channel_id=1, source_target_pairs={{0,1},{1,2},{2,3},{3,4},{4,5},{5,6},{6,7},{8,9},{9,10},{10,11},{11... | collective-permute-start | bytes 184328 | tf_op jit(solution)/shard_map/ppermute | solution.py:42
  218.6 1.6 copy-start.1
  218.6 1.6 copy-start.4
Sparse Core Ops, SparseCore 0:
  11.3 90.3 all-gather.2
where the time goes:
time: 288 us; the launch traced here: 284 us
  blocking collectives  89.1 us (31%)
  starting transfers between devices  50.8 us (18%)
  waiting for transfers between devices  50 us (17%)
  local copies, waits for them, and re-layouts  42.8 us (15%)
  other arithmetic  21.6 us (8%)
  between operations  18.2 us (6%)
  matrix products  11.7 us (4%)
    psum x4, blocking collectives, one_axis_at_a_time(): return functools.reduce(lax.psum, axes, x)  49.2 us
    all_gather x1, blocking collectives, side_by_side(): lax.all_gather(both, axis, axis=dim, tiled=True)  28.4 us
    all_to_all x1, waiting for transfers between devices, exchange_in_order(): whole = lax.all_to_all(whole, axes[k], k, k, tiled=True)  15.9 us
    ppermute x4, starting transfers between devices, padded_2(): before = lax.ppermute(last, axis, up)  13.9 us
    all_to_all x1, waiting for transfers between devices, per_device(): lax.all_to_all(flat, 'narrow', split_axis=1, concat_axis=0, tiled=True)  12.6 us
    all_to_all x1, blocking collectives, exchange_in_order(): whole = lax.all_to_all(whole, axes[k], k, k, tiled=True)  11.5 us
    all_to_all x1, starting transfers between devices, exchange_in_order(): whole = lax.all_to_all(whole, axes[k], k, k, tiled=True)  9.88 us
    ppermute x4, starting transfers between devices, padded_2(): after = lax.ppermute(leading, axis, down)  9.83 us
  transfers between devices with their start and end apart: 13, of which 8 were waited for; matrix products, arithmetic and copies ran while one was open for 14% of the time, Pallas kernels for 0%

commit v1 on v0

v1 whole, which is shorter than its diff:
```python
import functools

import jax
import jax.numpy as jnp
from jax import lax
from jax.experimental import pallas as pl
from jax.experimental.pallas import tpu as pltpu
from jax.sharding import PartitionSpec as P

MASS = (151.0 / 315.0, 397.0 / 1680.0, 1.0 / 42.0, 1.0 / 5040.0)
STIFF = (2.0 / 3.0, -0.125, -0.2, -1.0 / 120.0)
MESH = pl.DeviceIdType.MESH
NW, NN = 64, 8
CX, CY, NZ, NX = 10, 40, 320, 640
TILES = 100


def dot(a, b, ca, cb):
    return lax.dot_general(
        a,
        b,
        (((ca,), (cb,)), ((), ())),
        precision=lax.Precision.HIGHEST,
        preferred_element_type=jnp.float32,
    )


def has_second(v):
    return (lax.rem(v, 2) == 0) | (lax.rem(v, 16) == 1)


def second_tile(v):
    odd = lax.rem(v, 2)
    return 64 + (1 - odd) * lax.div(v, 2) + odd * (32 + lax.div(v, 16))


def band(coeffs):
    gap = jnp.abs(
        lax.broadcasted_iota(jnp.int32, (NZ, NZ), 0) - lax.broadcasted_iota(jnp.int32, (NZ, NZ), 1)
    )
    out = jnp.zeros((NZ, NZ), jnp.float32)
    for o in range(4):
        out = jnp.where(gap == o, coeffs[o], out)
    return out


def total(a, b):
    return jnp.sum(jnp.sum(a * b, axis=0, keepdims=True), axis=1, keepdims=True)


def stencil(padded, my, ky, first, second, bands, out):
    def along_y(p, carry):
        c = padded[p, 8:48, :]
        m = MASS[0] * c
        k = STIFF[0] * c
        for o in (1, 2, 3):
            s = padded[p, 8 - o : 48 - o, :] + padded[p, 8 + o : 48 + o, :]
            m += MASS[o] * s
            k += STIFF[o] * s
        my[p] = m
        ky[p] = k
        return carry

    lax.fori_loop(0, CX + 6, along_y, 0)

    def along_x(q, carry):
        a = my[q + 3]
        f = MASS[0] * a
        g = STIFF[0] * a + MASS[0] * ky[q + 3]
        for o in (1, 2, 3):
            s = my[q + 3 - o] + my[q + 3 + o]
            t = ky[q + 3 - o] + ky[q + 3 + o]
            f += MASS[o] * s
            g += STIFF[o] * s + MASS[o] * t
        first[q] = g
        second[q] = f
        return carry

    lax.fori_loop(0, CX, along_x, 0)
    g = first[...].reshape(CX * CY, NZ)
    f = second[...].reshape(CX * CY, NZ)
    out[...] = dot(g, bands[0], 1, 0) + dot(f, bands[1], 1, 0)


def kernel(
    ez_ref,
    sol_ref,
    res_ref,
    dir_ref,
    prev_ref,
    bx_ref,
    by_ref,
    bz_ref,
    ex_ref,
    ey_ref,
    sol_out,
    res_out,
    dir_out,
    wx,
    wy,
    wz,
    bands,
    exc,
    vd,
    vp,
    my,
    ky,
    first,
    second,
    image,
    fresh,
    n1s,
    n1r,
    lines,
    t2,
    s1,
    u0,
    u1,
    v0,
    v1,
    s2,
    n2s,
    n2r,
    red,
    rb1,
    rb2,
    lsem,
    wxs,
    wxr,
    wyzs,
    wyr,
    wzr,
    hs,
    hr,
    n1ss,
    n1rs,
    us0,
    us1,
    ur0,
    ur1,
    vs0,
    vs1,
    vr0,
    vr1,
    n2ss,
    n2rs,
    rs1,
    rr1,
    rs2,
    rr2,
):
    w = lax.axis_index("wide")
    n = lax.axis_index("narrow")
    wup, wdn = lax.rem(w + 1, NW), lax.rem(w + NW - 1, NW)
    nup, ndn = lax.rem(n + 1, NN), lax.rem(n + NN - 1, NN)
    barrier = pltpu.get_barrier_semaphore()

    for v in (vd, vp):
        for p in (0, 1, 2, 13, 14, 15):
            v[p] = jnp.zeros((56, NZ), jnp.float32)
        for p in range(3, 13):
            v[p, 0:8, :] = jnp.zeros((8, NZ), jnp.float32)
            v[p, 48:56, :] = jnp.zeros((8, NZ), jnp.float32)
    u1[...] = jnp.zeros_like(u1)

    def greet(d, carry):
        pl.semaphore_signal(
            barrier, inc=1, device_id={"wide": lax.rem(w + d, NW)}, device_id_type=MESH
        )
        return carry

    lax.fori_loop(1, NW, greet, 0)
    for d in range(1, NN):
        pl.semaphore_signal(
            barrier, inc=1, device_id={"narrow": lax.rem(n + d, NN)}, device_id_type=MESH
        )
    for a in (wup, wdn):
        for b in (nup, ndn):
            pl.semaphore_signal(
                barrier, inc=1, device_id={"wide": a, "narrow": b}, device_id_type=MESH
            )

    vd[3:13, 8:48, :] = dir_ref[...]
    bands[0] = band(MASS)
    bands[1] = band(STIFF)
    exc[...] = jnp.transpose(jnp.broadcast_to(ex_ref[...], (128, NX)))

    pl.semaphore_wait(barrier, NW - 1 + NN - 1 + 4)

    def send(src, dst, ssem, rsem, where):
        c = pltpu.make_async_remote_copy(
            src_ref=src,
            dst_ref=dst,
            send_sem=ssem,
            recv_sem=rsem,
            device_id=where,
            device_id_type=MESH,
        )
        c.start()

    def done(ref, sem):
        pltpu.make_async_copy(ref, ref, sem).wait()

    ownz = pltpu.make_async_copy(bz_ref, wz.at[pl.ds(n * CY, CY)], lsem.at[0])
    owny = pltpu.make_async_copy(by_ref, wy.at[pl.ds(n * CY, CY)], lsem.at[1])
    ownx = pltpu.make_async_copy(bx_ref, wx.at[w], lsem.at[2])
    ownz.start()
    owny.start()
    ownx.start()
    for d in range(1, NN):
        at = {"narrow": lax.rem(n + d, NN)}
        send(bz_ref, wz.at[pl.ds(n * CY, CY)], wyzs.at[0], wzr, at)
    for d in range(1, NN):
        at = {"narrow": lax.rem(n + d, NN)}
        send(by_ref, wy.at[pl.ds(n * CY, CY)], wyzs.at[1], wyr, at)

    has = {"xu": w < NW - 1, "xd": w > 0, "yu": n < NN - 1, "yd": n > 0}
    spans = {
        "": (pl.ds(3, 10), pl.ds(3, 10)),
        "xu": (pl.ds(10, 3), pl.ds(0, 3)),
        "xd": (pl.ds(3, 3), pl.ds(13, 3)),
    }
    rows = {
        "": (pl.ds(8, 40), pl.ds(8, 40)),
        "yu": (pl.ds(40, 8), pl.ds(0, 8)),
        "yd": (pl.ds(8, 8), pl.ds(48, 8)),
    }
    opposite = {"": "", "xu": "xd", "xd": "xu", "yu": "yd", "yd": "yu"}
    ways = [
        ("xu", ""),
        ("xd", ""),
        ("", "yu"),
        ("", "yd"),
        ("xu", "yu"),
        ("xu", "yd"),
        ("xd", "yu"),
        ("xd", "yd"),
    ]

    def exists(a, b):
        if a and b:
            return has[a] & has[b]
        return has[a or b]

    def start_halo(v, field):
        for i, (a, b) in enumerate(ways):

            @pl.when(exists(a, b))
            def _(i=i, a=a, b=b):
                at = {}
                if a:
                    at["wide"] = wup if a == "xu" else wdn
                if b:
                    at["narrow"] = nup if b == "yu" else ndn
                send(
                    v.at[spans[a][0], rows[b][0]],
                    v.at[spans[a][1], rows[b][1]],
                    hs.at[field, i],
                    hr.at[field, i],
                    at,
                )

    def wait_halo(v, field):
        for i, (a, b) in enumerate(ways):

            @pl.when(exists(opposite[a], opposite[b]))
            def _(i=i, a=a, b=b):
                done(v.at[spans[a][1], rows[b][1]], hr.at[field, i])

    def drain_halo(v, field):
        for i, (a, b) in enumerate(ways):

            @pl.when(exists(a, b))
            def _(i=i, a=a, b=b):
                done(v.at[spans[a][0], rows[b][0]], hs.at[field, i])

    start_halo(vd, 0)

    def send_wx(d, carry):
        send(bx_ref, wx.at[w], wxs, wxr, {"wide": lax.rem(w + d, NW)})
        return carry

    lax.fori_loop(1, NW, send_wx, 0)

    ownz.wait()
    done(wz.at[pl.ds(0, 280)], wzr)
    res2 = res_ref[...].reshape(CX * CY, NZ)
    n1s[...] = dot(wz[...], res2, 0, 1)
    own1 = pltpu.make_async_copy(n1s.at[pl.ds(n * CY, CY)], n1r.at[n], n1rs.at[n])
    own1.start()
    for d in range(1, NN):
        v = lax.rem(n + d, NN)
        send(n1s.at[pl.ds(v * CY, CY)], n1r.at[n], n1ss, n1rs.at[n], {"narrow": v})

    wait_halo(vd, 0)
    stencil(vd, my, ky, first, second, bands, image)

    for m in range(NN):
        done(n1r.at[m], n1rs.at[m])
        for x in range(CX):
            lines[x * CY : x * CY + CY, m * CY : m * CY + CY] = n1r[m, :, x * CY : x * CY + CY]

    owny.wait()
    done(wy.at[pl.ds(0, 280)], wyr)
    t2[...] = dot(lines[...], wy[...], 1, 0)
    for x in range(CX):
        for j in range(2):
            s1[pl.ds(j * 400 + x, 40, stride=10), :] = t2[
                x * CY : x * CY + CY, 128 * j : 128 * j + 128
            ]
        s1[pl.ds(800 + x, 20, stride=10), :] = jnp.concatenate(
            [t2[x * CY : x * CY + 20, 256:320], t2[x * CY + 20 : x * CY + CY, 256:320]], axis=1
        )

    mine2 = second_tile(w)
    two = has_second(w)
    one = jnp.logical_not(two)
    here = pl.ds(w * CX, CX)

    def send_u(d, carry):
        v = lax.rem(w + d, NW)
        send(s1.at[pl.ds(v * CX, CX)], u0.at[here], us0, ur0, {"wide": v})

        @pl.when(has_second(v))
        def _():
            send(s1.at[pl.ds(second_tile(v) * CX, CX)], u1.at[here], us1, ur1, {"wide": v})

        return carry

    lax.fori_loop(1, NW, send_u, 0)
    own_u0 = pltpu.make_async_copy(s1.at[here], u0.at[here], lsem.at[3])
    own_u0.start()

    @pl.when(two)
    def _():
        c = pltpu.make_async_copy(s1.at[pl.ds(mine2 * CX, CX)], u1.at[here], lsem.at[4])
        c.start()
        c.wait()

    def shift_row(t):
        j = lax.div(t, 40)
        c = t - j * 40
        row = jnp.where(j == 0, ey_ref[:, 0:128], ey_ref[:, 128:256])
        tail = ey_ref[:, 256:320]
        row = jnp.where(j == 2, jnp.concatenate([tail, tail], axis=1), row)
        late = c + 20 * lax.div(j, 2)
        low = lax.broadcasted_iota(jnp.int32, (1, 128), 1) < 64
        return row + jnp.where(low, ez_ref[n * CY + c], ez_ref[n * CY + late])

    shift = jnp.concatenate([shift_row(w), shift_row(mine2)], axis=1)
    ownx.wait()
    done(wx.at[pl.ds(0, 63)], wxr)
    full = wx[...].reshape(NX, NX)
    own_u0.wait()
    done(u0.at[pl.ds(0, 630)], ur0)

    @pl.when(two)
    def _():
        done(u1.at[pl.ds(0, 630)], ur1)

    both = jnp.concatenate([u0[...], u1[...]], axis=1)
    spectral = dot(full, both, 0, 0)
    cols = jnp.concatenate([exc[...], exc[...]], axis=1)
    inverse = dot(full, spectral / (cols + shift), 1, 0)
    v0[...] = inverse[:, 0:128]
    v1[...] = inverse[:, 128:256]

    def send_v(d, carry):
        v = lax.rem(w + d, NW)
        send(v0.at[pl.ds(v * CX, CX)], s2.at[here], vs0, vr0, {"wide": v})
        return carry

    lax.fori_loop(1, NW, send_v, 0)
    own_v0 = pltpu.make_async_copy(v0.at[here], s2.at[here], lsem.at[5])
    own_v0.start()
    there = pl.ds(mine2 * CX, CX)

    @pl.when(two)
    def _():
        def send_v1(d, carry):
            v = lax.rem(w + d, NW)
            send(v1.at[pl.ds(v * CX, CX)], s2.at[there], vs1, vr1, {"wide": v})
            return carry

        lax.fori_loop(1, NW, send_v1, 0)
        c = pltpu.make_async_copy(v1.at[here], s2.at[there], lsem.at[6])
        c.start()
        c.wait()

    own_v0.wait()
    done(s2.at[pl.ds(0, 630)], vr0)

    @pl.when(two)
    def _():
        done(s2.at[pl.ds(0, 350)], vr1)

    @pl.when(one)
    def _():
        done(s2.at[pl.ds(0, 360)], vr1)

    for x in range(CX):
        r = x * CY
        for j in range(2):
            t2[r : r + CY, 128 * j : 128 * j + 128] = s2[pl.ds(j * 400 + x, 40, stride=10), :]
        b = s2[pl.ds(800 + x, 20, stride=10), :]
        t2[r : r + 20, 256:320] = b[:, 0:64]
        t2[r + 20 : r + CY, 256:320] = b[:, 64:128]
    lines[...] = dot(t2[...], wy[...], 1, 1)
    for m in range(NN):
        for x in range(CX):
            n2s[m * CY : m * CY + CY, x * CY : x * CY + CY] = lines[
                x * CY : x * CY + CY, m * CY : m * CY + CY
            ]
    own2 = pltpu.make_async_copy(
        n2s.at[pl.ds(n * CY, CY)], n2r.at[pl.ds(n * CY, CY)], lsem.at[7]
    )
    own2.start()
    for d in range(1, NN):
        v = lax.rem(n + d, NN)
        send(n2s.at[pl.ds(v * CY, CY)], n2r.at[pl.ds(n * CY, CY)], n2ss, n2rs, {"narrow": v})
    own2.wait()
    done(n2r.at[pl.ds(0, 280)], n2rs)
    precond = dot(n2r[...], wz[...], 0, 1)
    vp[3:13, 8:48, :] = precond.reshape(CX, CY, NZ)
    start_halo(vp, 1)
    wait_halo(vp, 1)
    stencil(vp, my, ky, first, second, bands, fresh)

    precond = vp[3:13, 8:48, :].reshape(CX * CY, NZ)
    direction = dir_ref[...].reshape(CX * CY, NZ)
    res2 = res_ref[...].reshape(CX * CY, NZ)
    items = (
        total(res2, precond),
        total(precond, fresh[...]),
        total(precond, image[...]),
        total(direction, image[...]),
    )
    lane = lax.broadcasted_iota(jnp.int32, (1, 128), 1)
    row = jnp.zeros((1, 128), jnp.float32)
    for i, item in enumerate(items):
        row = jnp.where(lane == i, item, row)
    red[0] = row
    rb1[n] = row
    for d in range(1, NN):
        send(red.at[0], rb1.at[n], rs1, rr1, {"narrow": lax.rem(n + d, NN)})
    done(rb1.at[pl.ds(0, 7)], rr1)
    row = jnp.sum(rb1[...], axis=0)
    red[1] = row
    rb2[w] = row

    def send_r(d, carry):
        send(red.at[1], rb2.at[w], rs2, rr2, {"wide": lax.rem(w + d, NW)})
        return carry

    lax.fori_loop(1, NW, send_r, 0)
    done(rb2.at[pl.ds(0, 63)], rr2)
    row = jnp.sum(rb2[...], axis=0)
    now, self_term, cross, curvature = (
        jnp.sum(jnp.where(lane == i, row, 0.0), axis=1, keepdims=True) for i in range(4)
    )
    ratio = now / prev_ref[...]
    curvature = self_term + 2.0 * ratio * cross + ratio * ratio * curvature
    alpha = now / curvature
    direction = precond + ratio * direction
    new_image = fresh[...] + ratio * image[...]
    sol2 = sol_ref[...].reshape(CX * CY, NZ)
    dir_out[...] = direction.reshape(CX, CY, NZ)
    sol_out[...] = (sol2 + alpha * direction).reshape(CX, CY, NZ)
    res_out[...] = (res2 - alpha * new_image).reshape(CX, CY, NZ)

    for i in range(2):
        done(wz.at[pl.ds(0, 280)], wyzs.at[i])
    done(wx.at[pl.ds(0, 63)], wxs)
    drain_halo(vd, 0)
    drain_halo(vp, 1)
    done(n1s.at[pl.ds(0, 280)], n1ss)
    done(n2s.at[pl.ds(0, 280)], n2ss)
    done(s1.at[pl.ds(0, 630)], us0)
    done(v0.at[pl.ds(0, 630)], vs0)

    @pl.when(two)
    def _():
        done(s1.at[pl.ds(0, 350)], us1)
        done(v1.at[pl.ds(0, 630)], vs1)

    @pl.when(one)
    def _():
        done(s1.at[pl.ds(0, 360)], us1)

    done(rb1.at[pl.ds(0, 7)], rs1)
    done(rb2.at[pl.ds(0, 63)], rs2)


def per_device(sol, res, direction, prev, bx, by, bz, ex, ey, ez):
    f32 = jnp.float32
    brick = jax.ShapeDtypeStruct((CX, CY, NZ), f32)
    vmem = pl.BlockSpec(memory_space=pltpu.VMEM)
    smem = pl.BlockSpec(memory_space=pltpu.SMEM)
    dma = pltpu.SemaphoreType.DMA
    shapes = [
        (NW, CX, NX),
        (NZ, NZ),
        (NZ, NZ),
        (2, NZ, NZ),
        (NX, 128),
        (16, 56, NZ),
        (16, 56, NZ),
        (16, CY, NZ),
        (16, CY, NZ),
        (CX, CY, NZ),
        (CX, CY, NZ),
        (400, NZ),
        (400, NZ),
        (NZ, 400),
        (NN, CY, 400),
        (400, NZ),
        (400, NZ),
        (1000, 128),
        (NX, 128),
        (NX, 128),
        (NX, 128),
        (NX, 128),
        (1000, 128),
        (NZ, 400),
        (NZ, 400),
        (2, 1, 128),
        (NN, 1, 128),
        (NW, 1, 128),
    ]
    sems = [
        (8,),
        (),
        (),
        (2,),
        (),
        (),
        (2, 8),
        (2, 8),
        (),
        (8,),
        (),
        (),
        (),
        (),
        (),
        (),
        (),
        (),
        (),
        (),
        (),
        (),
        (),
        (),
    ]
    return pl.pallas_call(
        kernel,
        out_shape=(brick, brick, brick),
        in_specs=[smem] + [vmem] * 9,
        out_specs=(vmem, vmem, vmem),
        scratch_shapes=[pltpu.VMEM(s, f32) for s in shapes] + [dma(s) for s in sems],
        compiler_params=pltpu.CompilerParams(
            collective_id=0, has_side_effects=True, vmem_limit_bytes=56 << 20
        ),
        name="iterate",
    )(
        ez,
        sol,
        res,
        direction,
        prev.reshape(1, 1),
        bx,
        by,
        bz,
        ex.reshape(1, NX),
        ey.reshape(1, NZ),
    )


def solution(mesh):
    field = P("wide", "narrow", None)
    in_specs = (
        field,
        field,
        field,
        P(),
        P("wide", None),
        P("narrow", None),
        P("narrow", None),
        P(),
        P(),
        P(),
    )
    return jax.shard_map(
        per_device, mesh=mesh, in_specs=in_specs, out_specs=(field, field, field), check_vma=False
    )
```

time: 288 us -> 166 us (0.58); the launches traced: 284 us -> 165 us
  Pallas kernels: 0 us -> 159 us
  blocking collectives: 89.1 us -> 0 us
  starting transfers between devices: 50.8 us -> 0 us
  waiting for transfers between devices: 50 us -> 0 us
  local copies, waits for them, and re-layouts: 42.8 us -> 5.27 us
  other arithmetic: 21.6 us -> 0 us
  between operations: 18.2 us -> 1.34 us
  matrix products: 11.7 us -> 0 us
    pallas_call x0 -> x1, Pallas kernels: none -> 159 us  [per_device(): pl.pallas_call(kernel, out_shape=(brick, brick, brick), in_specs=[smem] +...]
    psum x4 -> x0, blocking collectives: 49.2 us -> none  [one_axis_at_a_time(): return functools.reduce(lax.psum, axes, x)]
    all_to_all x4 -> x0, waiting for transfers between devices: 31.3 us -> none  [the longest x1 15.9 us: exchange_in_order(): whole = lax.all_to_all(whole, axes[k], k, k, tiled=True)]
    all_gather x1 -> x0, blocking collectives: 28.4 us -> none  [side_by_side(): lax.all_gather(both, axis, axis=dim, tiled=True)]
    all_to_all x4 -> x0, starting transfers between devices: 27 us -> none  [the longest x1 9.88 us: exchange_in_order(): whole = lax.all_to_all(whole, axes[k], k, k, tiled=True)]
    ppermute x8 -> x0, starting transfers between devices: 23.7 us -> none  [the longest x4 13.9 us: padded_2(): before = lax.ppermute(last, axis, up)]
    ppermute x8 -> x0, waiting for transfers between devices: 18 us -> none  [the longest x4 9.31 us: padded_2(): before = lax.ppermute(last, axis, up)]
    add x8 -> x0, other arithmetic: 15 us -> none  [the longest x4 9.23 us: banded(): total + coeffs[offset] * lax.slice_in_dim(field, offset, offset + length,...]
  transfers between devices with their start and end apart: 13 -> 0, of which waited for: 8 -> 0; matrix products, arithmetic and copies ran while one was open for 14% -> 0% of each run, Pallas kernels for 0% -> 0%
where the time goes in v1:
time: 166 us; the launch traced here: 165 us
  Pallas kernels  159 us (96%)
  local copies, waits for them, and re-layouts  5.27 us (3%)
    pallas_call x1, Pallas kernels, per_device(): pl.pallas_call(kernel, out_shape=(brick, brick, brick), in_specs=[smem] +...  159 us
    unnamed x11, local copies, waits for them, and re-layouts  4.13 us

profile of v1, /device:TPU:1, one launch (start us, length us, event | category | flops | bytes accessed | tf_op | source)
XLA Modules:
  0.0 165.4 jit_solution(2431892092897196693)
XLA Ops:
  0.6 0.0 copy-start.3
  0.6 0.0 copy-start.2
  1.3 0.0 copy-done.3
  1.3 0.6 reshape.17.ey_ref
  1.9 0.0 copy-done.2
  1.9 0.6 reshape.16.ex_ref
  2.5 158.8 %iterate.1 = (f32[10,40,320]{2,1,0:T(8,128)}, f32[10,40,320]{2,1,0:T(8,128)}, f32[10,40,320]{2,1,0:T(8,128)}) custom-call(f32[320]{0:T(512)} %ez_ref.1, f32[10,40,320]{2,1,0:T(8,128)} %sol_ref.1, f32[10,40,320]{2,1,0:T(8,128)} %res_ref.1, f32[10,40,320]{2,1,0:T(8,128)} %dir_ref.1, f32[1,1]{1,0:T(1,128)} %bitcast.1.prev_ref, f32[10,640]{1,0:T(8,128)} %bx_ref.1, ...), custom_call_target="tpu_custom_call" | custom-call | tf_op jit(solution)/shard_map/iterate/pallas_call | solution.py:556
  161.2 0.0 copy-start.1
  161.2 2.0 %copy.17 = f32[10,40,320]{2,1,0:T(8,128)} copy(f32[10,40,320]{2,1,0:T(8,128)} %get-tuple-element.6) | data formatting | bytes 1024000
  163.2 0.0 copy-done.1
  163.2 0.0 copy-start
  163.2 0.8 copy.18
  164.1 0.5 copy-done
  164.5 0.8 copy.19
Async XLA Ops:
  0.6 0.7 copy-start.3
  0.6 1.3 copy-start.2
  161.2 2.0 %copy-start.1 = (f32[10,40,320]{2,1,0:T(8,128)S(1)}, f32[10,40,320]{2,1,0:T(8,128)}, u32[]{:S(2)}) copy-start(f32[10,40,320]{2,1,0:T(8,128)} %get-tuple-element.7) | copy-start | bytes 1536004
  163.2 1.3 copy-start

commit v2 on v1

--- a/solution.py
+++ b/solution.py
@@ -20,7 +20,7 @@
         a,
         b,
         (((ca,), (cb,)), ((), ())),
-        precision=lax.Precision.HIGHEST,
+        precision=lax.Precision.HIGH,
         preferred_element_type=jnp.float32,
     )
 
@@ -84,18 +84,18 @@
 
 def kernel(
     ez_ref,
-    sol_ref,
+    prev_ref,
+    ex_ref,
+    ey_ref,
     res_ref,
     dir_ref,
-    prev_ref,
     bx_ref,
     by_ref,
     bz_ref,
-    ex_ref,
-    ey_ref,
-    sol_out,
-    res_out,
-    dir_out,
+    pre_out,
+    img_out,
+    scal_out,
+    res,
     wx,
     wy,
     wz,
@@ -125,11 +125,16 @@
     rb1,
     rb2,
     lsem,
-    wxs,
-    wxr,
-    wyzs,
-    wyr,
-    wzr,
+    xs,
+    xr,
+    ybs,
+    ybr,
+    yfs,
+    yfr,
+    zbs,
+    zbr,
+    zfs,
+    zfr,
     hs,
     hr,
     n1ss,
@@ -153,7 +158,14 @@
     n = lax.axis_index("narrow")
     wup, wdn = lax.rem(w + 1, NW), lax.rem(w + NW - 1, NW)
     nup, ndn = lax.rem(n + 1, NN), lax.rem(n + NN - 1, NN)
+    core = lax.rem(w, 2)
+    sibling = w + 1 - 2 * core
+    gx, gy = lax.div(w, 16), lax.rem(lax.div(w, 2), 8)
     barrier = pltpu.get_barrier_semaphore()
+    get_res = pltpu.make_async_copy(res_ref, res, lsem.at[8])
+    get_dir = pltpu.make_async_copy(dir_ref, vd.at[pl.ds(3, CX), pl.ds(8, CY)], lsem.at[9])
+    get_res.start()
+    get_dir.start()
 
     for v in (vd, vp):
         for p in (0, 1, 2, 13, 14, 15):
@@ -180,10 +192,9 @@
                 barrier, inc=1, device_id={"wide": a, "narrow": b}, device_id_type=MESH
             )
 
-    vd[3:13, 8:48, :] = dir_ref[...]
     bands[0] = band(MASS)
     bands[1] = band(STIFF)
-    exc[...] = jnp.transpose(jnp.broadcast_to(ex_ref[...], (128, NX)))
+    exc[...] = jnp.transpose(jnp.broadcast_to(ex_ref[...].reshape(1, NX), (128, NX)))
 
     pl.semaphore_wait(barrier, NW - 1 + NN - 1 + 4)
 
@@ -201,18 +212,50 @@
     def done(ref, sem):
         pltpu.make_async_copy(ref, ref, sem).wait()
 
-    ownz = pltpu.make_async_copy(bz_ref, wz.at[pl.ds(n * CY, CY)], lsem.at[0])
-    owny = pltpu.make_async_copy(by_ref, wy.at[pl.ds(n * CY, CY)], lsem.at[1])
-    ownx = pltpu.make_async_copy(bx_ref, wx.at[w], lsem.at[2])
+    def near(d):
+        return core == (d + 1) % 2
+
+    def rows_of(v):
+        return pl.ds(pl.multiple_of(v * CY, 8), CY)
+
+    def share(own, whole, ssem, rsem):
+        for d in range(1, NN):
+
+            @pl.when(near(d))
+            def _(d=d):
+                at = {"narrow": lax.rem(n + d, NN)}
+                send(own, whole.at[rows_of(n)], ssem, rsem.at[d], at)
+
+    def hand_over(whole, rsem, fsem, gsem):
+        for d in range(1, NN):
+
+            @pl.when(near(d))
+            def _(d=d):
+                m = rows_of(lax.rem(n + NN - d, NN))
+                done(whole.at[m], rsem.at[d])
+                send(whole.at[m], whole.at[m], fsem, gsem, {"wide": sibling})
+
+    def by_core(whole, sem, first_rows):
+        @pl.when(core == 0)
+        def _():
+            done(whole.at[pl.ds(0, first_rows)], sem)
+
+        @pl.when(core == 1)
+        def _():
+            done(whole.at[pl.ds(0, 280 - first_rows)], sem)
+
+    ownz = pltpu.make_async_copy(bz_ref, wz.at[rows_of(n)], lsem.at[0])
+    owny = pltpu.make_async_copy(by_ref, wy.at[rows_of(n)], lsem.at[1])
+    ownx = pltpu.make_async_copy(bx_ref, wx.at[gx, gy, core], lsem.at[2])
     ownz.start()
     owny.start()
     ownx.start()
-    for d in range(1, NN):
-        at = {"narrow": lax.rem(n + d, NN)}
-        send(bz_ref, wz.at[pl.ds(n * CY, CY)], wyzs.at[0], wzr, at)
-    for d in range(1, NN):
-        at = {"narrow": lax.rem(n + d, NN)}
-        send(by_ref, wy.at[pl.ds(n * CY, CY)], wyzs.at[1], wyr, at)
+    share(bz_ref, wz, zbs, zbr)
+    share(by_ref, wy, ybs, ybr)
+
+    for d in range(1, 8):
+        at = {"wide": gx * 16 + lax.rem(gy + d, 8) * 2 + core}
+        send(bx_ref, wx.at[gx, gy, core], xs.at[0], xr.at[0], at)
 
     has = {"xu": w < NW - 1, "xd": w > 0, "yu": n < NN - 1, "yd": n > 0}
     spans = {
@@ -274,17 +317,11 @@
             def _(i=i, a=a, b=b):
                 done(v.at[spans[a][0], rows[b][0]], hs.at[field, i])
 
-    start_halo(vd, 0)
-
-    def send_wx(d, carry):
-        send(bx_ref, wx.at[w], wxs, wxr, {"wide": lax.rem(w + d, NW)})
-        return carry
-
-    lax.fori_loop(1, NW, send_wx, 0)
-
+    hand_over(wz, zbr, zfs, zfr)
+    get_res.wait()
+    res2 = res[...].reshape(CX * CY, NZ)
     ownz.wait()
-    done(wz.at[pl.ds(0, 280)], wzr)
-    res2 = res_ref[...].reshape(CX * CY, NZ)
+    by_core(wz, zfr, 120)
     n1s[...] = dot(wz[...], res2, 0, 1)
     own1 = pltpu.make_async_copy(n1s.at[pl.ds(n * CY, CY)], n1r.at[n], n1rs.at[n])
     own1.start()
@@ -292,8 +329,14 @@
         v = lax.rem(n + d, NN)
         send(n1s.at[pl.ds(v * CY, CY)], n1r.at[n], n1ss, n1rs.at[n], {"narrow": v})
 
-    wait_halo(vd, 0)
-    stencil(vd, my, ky, first, second, bands, image)
+    hand_over(wy, ybr, yfs, yfr)
+    get_dir.wait()
+    start_halo(vd, 0)
+    ownx.wait()
+    done(wx.at[0, pl.ds(0, 7), 0], xr.at[0])
+    for e in range(1, 4):
+        at = {"wide": lax.rem(gx + e, 4) * 16 + gy * 2 + core}
+        send(wx.at[gx, :, core], wx.at[gx, :, core], xs.at[1], xr.at[1], at)
 
     for m in range(NN):
         done(n1r.at[m], n1rs.at[m])
@@ -301,7 +344,7 @@
             lines[x * CY : x * CY + CY, m * CY : m * CY + CY] = n1r[m, :, x * CY : x * CY + CY]
 
     owny.wait()
-    done(wy.at[pl.ds(0, 280)], wyr)
+    by_core(wy, yfr, 120)
     t2[...] = dot(lines[...], wy[...], 1, 0)
     for x in range(CX):
         for j in range(2):
@@ -337,19 +380,26 @@
         c.start()
         c.wait()
 
+    ey = ey_ref[...].reshape(1, NZ)
+
     def shift_row(t):
         j = lax.div(t, 40)
         c = t - j * 40
-        row = jnp.where(j == 0, ey_ref[:, 0:128], ey_ref[:, 128:256])
-        tail = ey_ref[:, 256:320]
+        row = jnp.where(j == 0, ey[:, 0:128], ey[:, 128:256])
+        tail = ey[:, 256:320]
         row = jnp.where(j == 2, jnp.concatenate([tail, tail], axis=1), row)
         late = c + 20 * lax.div(j, 2)
         low = lax.broadcasted_iota(jnp.int32, (1, 128), 1) < 64
         return row + jnp.where(low, ez_ref[n * CY + c], ez_ref[n * CY + late])
 
     shift = jnp.concatenate([shift_row(w), shift_row(mine2)], axis=1)
-    ownx.wait()
-    done(wx.at[pl.ds(0, 63)], wxr)
+    done(wx.at[pl.ds(0, 3), :, 0], xr.at[1])
+    send(wx.at[:, :, core], wx.at[:, :, core], xs.at[2], xr.at[2], {"wide": sibling})
+
+    wait_halo(vd, 0)
+    stencil(vd, my, ky, first, second, bands, image)
+
+    done(wx.at[:, :, 0], xr.at[2])
     full = wx[...].reshape(NX, NX)
     own_u0.wait()
     done(u0.at[pl.ds(0, 630)], ur0)
@@ -427,8 +477,8 @@
     stencil(vp, my, ky, first, second, bands, fresh)
 
     precond = vp[3:13, 8:48, :].reshape(CX * CY, NZ)
-    direction = dir_ref[...].reshape(CX * CY, NZ)
-    res2 = res_ref[...].reshape(CX * CY, NZ)
+    direction = vd[3:13, 8:48, :].reshape(CX * CY, NZ)
+    res2 = res[...].reshape(CX * CY, NZ)
     items = (
         total(res2, precond),
         total(precond, fresh[...]),
@@ -458,19 +508,20 @@
     now, self_term, cross, curvature = (
         jnp.sum(jnp.where(lane == i, row, 0.0), axis=1, keepdims=True) for i in range(4)
     )
-    ratio = now / prev_ref[...]
+    ratio = now / prev_ref[0]
     curvature = self_term + 2.0 * ratio * cross + ratio * ratio * curvature
     alpha = now / curvature
-    direction = precond + ratio * direction
-    new_image = fresh[...] + ratio * image[...]
-    sol2 = sol_ref[...].reshape(CX * CY, NZ)
-    dir_out[...] = direction.reshape(CX, CY, NZ)
-    sol_out[...] = (sol2 + alpha * direction).reshape(CX, CY, NZ)
-    res_out[...] = (res2 - alpha * new_image).reshape(CX, CY, NZ)
-
-    for i in range(2):
-        done(wz.at[pl.ds(0, 280)], wyzs.at[i])
-    done(wx.at[pl.ds(0, 63)], wxs)
+    pre_out[...] = precond.reshape(CX, CY, NZ)
+    img_out[...] = (fresh[...] + ratio * image[...]).reshape(CX, CY, NZ)
+    scal_out[...] = jnp.where(lane == 0, ratio, alpha)
+
+    by_core(wz, zbs, 160)
+    by_core(wz, zfs, 160)
+    by_core(wy, ybs, 160)
+    by_core(wy, yfs, 160)
+    done(wx.at[0, pl.ds(0, 7), 0], xs.at[0])
+    done(wx.at[pl.ds(0, 3), :, 0], xs.at[1])
+    done(wx.at[:, :, 0], xs.at[2])
     drain_halo(vd, 0)
     drain_halo(vp, 1)
     done(n1s.at[pl.ds(0, 280)], n1ss)
@@ -496,9 +547,11 @@
     brick = jax.ShapeDtypeStruct((CX, CY, NZ), f32)
     vmem = pl.BlockSpec(memory_space=pltpu.VMEM)
     smem = pl.BlockSpec(memory_space=pltpu.SMEM)
+    hbm = pl.BlockSpec(memory_space=pltpu.HBM)
     dma = pltpu.SemaphoreType.DMA
     shapes = [
-        (NW, CX, NX),
+        (CX, CY, NZ),
+        (4, 8, 2, CX, NX),
         (NZ, NZ),
         (NZ, NZ),
         (2, NZ, NZ),
@@ -527,54 +580,22 @@
         (NN, 1, 128),
         (NW, 1, 128),
     ]
-    sems = [
-        (8,),
-        (),
-        (),
-        (2,),
-        (),
-        (),
-        (2, 8),
-        (2, 8),
-        (),
-        (8,),
-        (),
-        (),
-        (),
-        (),
-        (),
-        (),
-        (),
-        (),
-        (),
-        (),
-        (),
-        (),
-        (),
-        (),
-    ]
-    return pl.pallas_call(
+    sems = [(10,), (3,), (3,), (), (8,), (), (), (), (8,), (), ()]
+    sems += [(2, 8), (2, 8), (), (8,)] + [()] * 14
+    precond, image, scal = pl.pallas_call(
         kernel,
-        out_shape=(brick, brick, brick),
-        in_specs=[smem] + [vmem] * 9,
+        out_shape=(brick, brick, jax.ShapeDtypeStruct((1, 128), f32)),
+        in_specs=[smem, smem, vmem, vmem] + [hbm] * 5,
         out_specs=(vmem, vmem, vmem),
         scratch_shapes=[pltpu.VMEM(s, f32) for s in shapes] + [dma(s) for s in sems],
         compiler_params=pltpu.CompilerParams(
             collective_id=0, has_side_effects=True, vmem_limit_bytes=56 << 20
         ),
         name="iterate",
-    )(
-        ez,
-        sol,
-        res,
-        direction,
-        prev.reshape(1, 1),
-        bx,
-        by,
-        bz,
-        ex.reshape(1, NX),
-        ey.reshape(1, NZ),
-    )
+    )(ez, prev, ex, ey, res, direction, bx, by, bz)
+    ratio, alpha = scal[0, 0], scal[0, 1]
+    direction = precond + ratio * direction
+    return sol + alpha * direction, res - alpha * image, direction
 
 
 def solution(mesh):

time: 166 us -> 131 us (0.79)
  Pallas kernels: 159 us -> 124 us
  other arithmetic: 0 us -> 4.1 us
  local copies, waits for them, and re-layouts: 5.27 us -> 1.25 us
    pallas_call x1, Pallas kernels: 159 us -> 124 us  [per_device(): pl.pallas_call(kernel, out_shape=(brick, brick, jax.ShapeDtypeStruct((1,...]
    add x0 -> x1, other arithmetic: none -> 4.1 us  [per_device(): return (sol + alpha * direction, res - alpha * image, direction)]
    unnamed x11 -> x6, local copies, waits for them, and re-layouts: 4.13 us -> 0.67 us
where the time goes in v2:
time: 131 us
  Pallas kernels  124 us (95%)
  other arithmetic  4.1 us (3%)
  between operations  1.31 us (1%)
    pallas_call x1, Pallas kernels, per_device(): pl.pallas_call(kernel, out_shape=(brick, brick, jax.ShapeDtypeStruct((1,...  124 us
    add x1, other arithmetic, per_device(): return (sol + alpha * direction, res - alpha * image, direction)  4.1 us

profile of v2, /device:TPU:1, one launch (start us, length us, event | category | flops | bytes accessed | tf_op | source)
XLA Modules:
  0.0 130.5 jit_solution(5815951255173842740)
XLA Ops:
  1.3 0.0 copy-start
  1.3 0.0 copy-start.1
  1.3 123.8 %iterate.1 = (f32[10,40,320]{2,1,0:T(8,128)}, f32[10,40,320]{2,1,0:T(8,128)}, f32[1,128]{1,0:T(1,128)}) custom-call(f32[320]{0:T(512)} %ez_ref.1, f32[1]{0:T(128)S(6)} %copy.13.prev_ref, f32[640]{0:T(1024)} %ex_ref.1, f32[320]{0:T(512)} %ey_ref.1, f32[10,40,320]{2,1,0:T(8,128)} %res_ref.1, f32[10,40,320]{2,1,0:T(8,128)} %dir_ref.1, f32[10,640]{1,0:T(8,128)} %bx_ref.1, ...), custom_call_target="tpu_custom_call" | custom-call | tf_op jit(solution)/shard_map/iterate/pallas_call | solution.py:585
  125.1 0.0 copy-start.2
  125.2 0.7 copy-done.2
  125.8 0.6 fusion
  126.4 0.0 copy-done
  126.4 0.0 copy-done.1
  126.4 4.1 %multiply_add_fusion = (f32[10,40,320]{2,1,0:T(8,128)}, f32[10,40,320]{2,1,0:T(8,128)}, f32[10,40,320]{2,1,0:T(8,128)}) fusion(f32[10,40,320]{2,1,0:T(8,128)} %param.10, f32[]{:T(128)} %bitcast, f32[10,40,320]{2,1,0:T(8,128)} %get-tuple-element.7, f32[10,40,320]{2,1,0:T(8,128)S(1)} %copy-done.1, f32[]{:T(128)} %bitcast.1, f32[10,40,320]{2,1,0:T(8,128)S(1)} %copy-done, ...), kind=kLoop, calls=%fused_computation.1 | loop fusion | flops 768000 | bytes 4096008 | tf_op jit(solution)/shard_map/add | solution.py:598
Async XLA Ops:
  1.3 125.1 %copy-start = (f32[10,40,320]{2,1,0:T(8,128)S(1)}, f32[10,40,320]{2,1,0:T(8,128)}, u32[]{:S(2)}) copy-start(f32[10,40,320]{2,1,0:T(8,128)} %res_ref.1) | copy-start | bytes 1536004
  1.3 125.1 %copy-start.1 = (f32[10,40,320]{2,1,0:T(8,128)S(1)}, f32[10,40,320]{2,1,0:T(8,128)}, u32[]{:S(2)}) copy-start(f32[10,40,320]{2,1,0:T(8,128)} %dir_ref.1) | copy-start | bytes 1536004
  125.1 0.7 copy-start.2

commit v3 on v2

--- a/solution.py
+++ b/solution.py
@@ -12,7 +12,7 @@
 MESH = pl.DeviceIdType.MESH
 NW, NN = 64, 8
 CX, CY, NZ, NX = 10, 40, 320, 640
-TILES = 100
+CHUNKS = ((0, 5), (5, 5))
 
 
 def dot(a, b, ca, cb):
@@ -83,18 +83,23 @@
 
 
 def kernel(
-    ez_ref,
     prev_ref,
-    ex_ref,
-    ey_ref,
+    ex_hbm,
+    ey_hbm,
+    ez_hbm,
+    sol_ref,
     res_ref,
     dir_ref,
     bx_ref,
     by_ref,
     bz_ref,
-    pre_out,
-    img_out,
-    scal_out,
+    sol_out,
+    res_out,
+    dir_out,
+    ex_ref,
+    ey_ref,
+    ez_ref,
+    sol,
     res,
     wx,
     wy,
@@ -111,6 +116,7 @@
     fresh,
     n1s,
     n1r,
+    wxp,
     lines,
     t2,
     s1,
@@ -164,8 +170,15 @@
     barrier = pltpu.get_barrier_semaphore()
     get_res = pltpu.make_async_copy(res_ref, res, lsem.at[8])
     get_dir = pltpu.make_async_copy(dir_ref, vd.at[pl.ds(3, CX), pl.ds(8, CY)], lsem.at[9])
-    get_res.start()
-    get_dir.start()
+    get_sol = pltpu.make_async_copy(sol_ref, sol, lsem.at[10])
+    small = [
+        pltpu.make_async_copy(a, b, lsem.at[11 + i])
+        for i, (a, b) in enumerate(
+            ((ex_hbm, ex_ref), (ey_hbm, ey_ref), (ez_hbm, ez_ref))
+        )
+    ]
+    for c in [get_res, get_dir, *small, get_sol]:
+        c.start()
 
     for v in (vd, vp):
         for p in (0, 1, 2, 13, 14, 15):
@@ -194,6 +207,8 @@
 
     bands[0] = band(MASS)
     bands[1] = band(STIFF)
+    for c in small:
+        c.wait()
     exc[...] = jnp.transpose(jnp.broadcast_to(ex_ref[...].reshape(1, NX), (128, NX)))
 
     pl.semaphore_wait(barrier, NW - 1 + NN - 1 + 4)
@@ -319,15 +334,15 @@
 
     hand_over(wz, zbr, zfs, zfr)
     get_res.wait()
-    res2 = res[...].reshape(CX * CY, NZ)
     ownz.wait()
     by_core(wz, zfr, 120)
-    n1s[...] = dot(wz[...], res2, 0, 1)
-    own1 = pltpu.make_async_copy(n1s.at[pl.ds(n * CY, CY)], n1r.at[n], n1rs.at[n])
-    own1.start()
-    for d in range(1, NN):
-        v = lax.rem(n + d, NN)
-        send(n1s.at[pl.ds(v * CY, CY)], n1r.at[n], n1ss, n1rs.at[n], {"narrow": v})
+    for i, (x0, p) in enumerate(CHUNKS):
+        n1s[i][...] = dot(wz[...], res[x0 : x0 + p].reshape(p * CY, NZ), 0, 1)
+        pltpu.make_async_copy(n1s[i].at[rows_of(n)], n1r[i].at[n], n1rs.at[i, n]).start()
+        for d in range(1, NN):
+            v = lax.rem(n + d, NN)
+            at = {"narrow": v}
+            send(n1s[i].at[rows_of(v)], n1r[i].at[n], n1ss.at[i], n1rs.at[i, n], at)
 
     hand_over(wy, ybr, yfs, yfr)
     get_dir.wait()
@@ -338,47 +353,56 @@
         at = {"wide": lax.rem(gx + e, 4) * 16 + gy * 2 + core}
         send(wx.at[gx, :, core], wx.at[gx, :, core], xs.at[1], xr.at[1], at)
 
-    for m in range(NN):
-        done(n1r.at[m], n1rs.at[m])
-        for x in range(CX):
-            lines[x * CY : x * CY + CY, m * CY : m * CY + CY] = n1r[m, :, x * CY : x * CY + CY]
-
-    owny.wait()
-    by_core(wy, yfr, 120)
-    t2[...] = dot(lines[...], wy[...], 1, 0)
-    for x in range(CX):
-        for j in range(2):
-            s1[pl.ds(j * 400 + x, 40, stride=10), :] = t2[
-                x * CY : x * CY + CY, 128 * j : 128 * j + 128
-            ]
-        s1[pl.ds(800 + x, 20, stride=10), :] = jnp.concatenate(
-            [t2[x * CY : x * CY + 20, 256:320], t2[x * CY + 20 : x * CY + CY, 256:320]], axis=1
-        )
-
     mine2 = second_tile(w)
     two = has_second(w)
     one = jnp.logical_not(two)
-    here = pl.ds(w * CX, CX)
-
-    def send_u(d, carry):
-        v = lax.rem(w + d, NW)
-        send(s1.at[pl.ds(v * CX, CX)], u0.at[here], us0, ur0, {"wide": v})
-
-        @pl.when(has_second(v))
-        def _():
-            send(s1.at[pl.ds(second_tile(v) * CX, CX)], u1.at[here], us1, ur1, {"wide": v})
-
-        return carry
-
-    lax.fori_loop(1, NW, send_u, 0)
-    own_u0 = pltpu.make_async_copy(s1.at[here], u0.at[here], lsem.at[3])
-    own_u0.start()
-
-    @pl.when(two)
-    def _():
-        c = pltpu.make_async_copy(s1.at[pl.ds(mine2 * CX, CX)], u1.at[here], lsem.at[4])
-        c.start()
-        c.wait()
+
+    for i, (x0, p) in enumerate(CHUNKS):
+        for m in range(NN):
+            done(n1r[i].at[m], n1rs.at[i, m])
+            for x in range(p):
+                r = (x0 + x) * CY
+                lines[r : r + CY, m * CY : m * CY + CY] = n1r[i][m, :, x * CY : x * CY + CY]
+        if i == 0:
+            owny.wait()
+            by_core(wy, yfr, 120)
+        span = slice(x0 * CY, (x0 + p) * CY)
+        t2[span, :] = dot(lines[span, :], wy[...], 1, 0)
+        for x in range(x0, x0 + p):
+            r = x * CY
+            for j in range(2):
+                s1[pl.ds(j * 400 + x, 40, stride=10), :] = t2[
+                    r : r + CY, 128 * j : 128 * j + 128
+                ]
+            s1[pl.ds(800 + x, 20, stride=10), :] = jnp.concatenate(
+                [t2[r : r + 20, 256:320], t2[r + 20 : r + CY, 256:320]], axis=1
+            )
+        here = pl.ds(64 * x0 + w * p, p)
+
+        def send_u(d, carry, i=i, x0=x0, p=p, here=here):
+            v = lax.rem(w + d, NW)
+            at = {"wide": v}
+            send(s1.at[pl.ds(v * CX + x0, p)], u0.at[here], us0.at[i], ur0.at[i], at)
+
+            @pl.when(has_second(v))
+            def _():
+                src = s1.at[pl.ds(second_tile(v) * CX + x0, p)]
+                send(src, u1.at[here], us1.at[i], ur1.at[i], at)
+
+            return carry
+
+        lax.fori_loop(1, NW, send_u, 0, unroll=3)
+        own = pltpu.make_async_copy(s1.at[pl.ds(w * CX + x0, p)], u0.at[here], lsem.at[3])
+        own.start()
+        own.wait()
+
+        @pl.when(two)
+        def _(x0=x0, p=p, here=here):
+            c = pltpu.make_async_copy(
+                s1.at[pl.ds(mine2 * CX + x0, p)], u1.at[here], lsem.at[4]
+            )
+            c.start()
+            c.wait()
 
     ey = ey_ref[...].reshape(1, NZ)
 
@@ -395,83 +419,94 @@
     shift = jnp.concatenate([shift_row(w), shift_row(mine2)], axis=1)
     done(wx.at[pl.ds(0, 3), :, 0], xr.at[1])
     send(wx.at[:, :, core], wx.at[:, :, core], xs.at[2], xr.at[2], {"wide": sibling})
-
     wait_halo(vd, 0)
     stencil(vd, my, ky, first, second, bands, image)
 
     done(wx.at[:, :, 0], xr.at[2])
-    full = wx[...].reshape(NX, NX)
-    own_u0.wait()
-    done(u0.at[pl.ds(0, 630)], ur0)
-
-    @pl.when(two)
-    def _():
-        done(u1.at[pl.ds(0, 630)], ur1)
+    for x0, p in CHUNKS:
+        wxp[64 * x0 : 64 * (x0 + p), :] = wx[:, :, :, x0 : x0 + p, :].reshape(64 * p, NX)
+    for i, (x0, p) in enumerate(CHUNKS):
+        done(u0.at[pl.ds(0, 63 * p)], ur0.at[i])
+
+        @pl.when(two)
+        def _(i=i, p=p):
+            done(u1.at[pl.ds(0, 63 * p)], ur1.at[i])
 
     both = jnp.concatenate([u0[...], u1[...]], axis=1)
-    spectral = dot(full, both, 0, 0)
+    spectral = dot(wxp[...], both, 0, 0)
     cols = jnp.concatenate([exc[...], exc[...]], axis=1)
-    inverse = dot(full, spectral / (cols + shift), 1, 0)
-    v0[...] = inverse[:, 0:128]
-    v1[...] = inverse[:, 128:256]
-
-    def send_v(d, carry):
-        v = lax.rem(w + d, NW)
-        send(v0.at[pl.ds(v * CX, CX)], s2.at[here], vs0, vr0, {"wide": v})
-        return carry
-
-    lax.fori_loop(1, NW, send_v, 0)
-    own_v0 = pltpu.make_async_copy(v0.at[here], s2.at[here], lsem.at[5])
-    own_v0.start()
-    there = pl.ds(mine2 * CX, CX)
-
-    @pl.when(two)
-    def _():
-        def send_v1(d, carry):
+    spectral = spectral / (cols + shift)
+    for i, (x0, p) in enumerate(CHUNKS):
+        span = slice(64 * x0, 64 * (x0 + p))
+        inverse = dot(wxp[span, :], spectral, 1, 0)
+        v0[span, :] = inverse[:, 0:128]
+        v1[span, :] = inverse[:, 128:256]
+        mine = pl.ds(64 * x0 + w * p, p)
+        here = pl.ds(w * CX + x0, p)
+        there = pl.ds(mine2 * CX + x0, p)
+
+        def send_v(d, carry, i=i, x0=x0, p=p, here=here):
             v = lax.rem(w + d, NW)
-            send(v1.at[pl.ds(v * CX, CX)], s2.at[there], vs1, vr1, {"wide": v})
+            src = v0.at[pl.ds(64 * x0 + v * p, p)]
+            send(src, s2.at[here], vs0.at[i], vr0.at[i], {"wide": v})
             return carry
 
-        lax.fori_loop(1, NW, send_v1, 0)
-        c = pltpu.make_async_copy(v1.at[here], s2.at[there], lsem.at[6])
-        c.start()
-        c.wait()
-
-    own_v0.wait()
-    done(s2.at[pl.ds(0, 630)], vr0)
-
-    @pl.when(two)
-    def _():
-        done(s2.at[pl.ds(0, 350)], vr1)
-
-    @pl.when(one)
-    def _():
-        done(s2.at[pl.ds(0, 360)], vr1)
-
-    for x in range(CX):
-        r = x * CY
-        for j in range(2):
-            t2[r : r + CY, 128 * j : 128 * j + 128] = s2[pl.ds(j * 400 + x, 40, stride=10), :]
-        b = s2[pl.ds(800 + x, 20, stride=10), :]
-        t2[r : r + 20, 256:320] = b[:, 0:64]
-        t2[r + 20 : r + CY, 256:320] = b[:, 64:128]
-    lines[...] = dot(t2[...], wy[...], 1, 1)
-    for m in range(NN):
-        for x in range(CX):
-            n2s[m * CY : m * CY + CY, x * CY : x * CY + CY] = lines[
-                x * CY : x * CY + CY, m * CY : m * CY + CY
-            ]
-    own2 = pltpu.make_async_copy(
-        n2s.at[pl.ds(n * CY, CY)], n2r.at[pl.ds(n * CY, CY)], lsem.at[7]
-    )
-    own2.start()
-    for d in range(1, NN):
-        v = lax.rem(n + d, NN)
-        send(n2s.at[pl.ds(v * CY, CY)], n2r.at[pl.ds(n * CY, CY)], n2ss, n2rs, {"narrow": v})
-    own2.wait()
-    done(n2r.at[pl.ds(0, 280)], n2rs)
-    precond = dot(n2r[...], wz[...], 0, 1)
-    vp[3:13, 8:48, :] = precond.reshape(CX, CY, NZ)
+        lax.fori_loop(1, NW, send_v, 0, unroll=3)
+        own = pltpu.make_async_copy(v0.at[mine], s2.at[here], lsem.at[5])
+        own.start()
+        own.wait()
+
+        @pl.when(two)
+        def _(i=i, x0=x0, p=p, there=there, mine=mine):
+            def send_v1(d, carry):
+                v = lax.rem(w + d, NW)
+                src = v1.at[pl.ds(64 * x0 + v * p, p)]
+                send(src, s2.at[there], vs1.at[i], vr1.at[i], {"wide": v})
+                return carry
+
+            lax.fori_loop(1, NW, send_v1, 0, unroll=3)
+            c = pltpu.make_async_copy(v1.at[mine], s2.at[there], lsem.at[6])
+            c.start()
+            c.wait()
+
+    for i, (x0, p) in enumerate(CHUNKS):
+        done(s2.at[pl.ds(0, 63 * p)], vr0.at[i])
+
+        @pl.when(two)
+        def _(i=i, p=p):
+            done(s2.at[pl.ds(0, 35 * p)], vr1.at[i])
+
+        @pl.when(one)
+        def _(i=i, p=p):
+            done(s2.at[pl.ds(0, 36 * p)], vr1.at[i])
+
+        for x in range(x0, x0 + p):
+            r = x * CY
+            for j in range(2):
+                t2[r : r + CY, 128 * j : 128 * j + 128] = s2[pl.ds(j * 400 + x, 40, stride=10), :]
+            b = s2[pl.ds(800 + x, 20, stride=10), :]
+            t2[r : r + 20, 256:320] = b[:, 0:64]
+            t2[r + 20 : r + CY, 256:320] = b[:, 64:128]
+        span = slice(x0 * CY, (x0 + p) * CY)
+        lines[span, :] = dot(t2[span, :], wy[...], 1, 1)
+        for m in range(NN):
+            for x in range(p):
+                r = (x0 + x) * CY
+                n2s[i][m * CY : m * CY + CY, x * CY : x * CY + CY] = lines[
+                    r : r + CY, m * CY : m * CY + CY
+                ]
+        own = pltpu.make_async_copy(n2s[i].at[rows_of(n)], n2r[i].at[rows_of(n)], lsem.at[7])
+        own.start()
+        for d in range(1, NN):
+            v = lax.rem(n + d, NN)
+            at = {"narrow": v}
+            send(n2s[i].at[rows_of(v)], n2r[i].at[rows_of(n)], n2ss.at[i], n2rs.at[i], at)
+        own.wait()
+
+    for i, (x0, p) in enumerate(CHUNKS):
+        done(n2r[i].at[pl.ds(0, 280)], n2rs.at[i])
+        piece = dot(n2r[i][...], wz[...], 0, 1).reshape(p, CY, NZ)
+        vp[3 + x0 : 3 + x0 + p, 8:48, :] = piece
     start_halo(vp, 1)
     wait_halo(vp, 1)
     stencil(vp, my, ky, first, second, bands, fresh)
@@ -511,9 +546,13 @@
     ratio = now / prev_ref[0]
     curvature = self_term + 2.0 * ratio * cross + ratio * ratio * curvature
     alpha = now / curvature
-    pre_out[...] = precond.reshape(CX, CY, NZ)
-    img_out[...] = (fresh[...] + ratio * image[...]).reshape(CX, CY, NZ)
-    scal_out[...] = jnp.where(lane == 0, ratio, alpha)
+    get_sol.wait()
+    sol2 = sol[...].reshape(CX * CY, NZ)
+    direction = precond + ratio * direction
+    new_image = fresh[...] + ratio * image[...]
+    sol_out[...] = (sol2 + alpha * direction).reshape(CX, CY, NZ)
+    res_out[...] = (res2 - alpha * new_image).reshape(CX, CY, NZ)
+    dir_out[...] = direction.reshape(CX, CY, NZ)
 
     by_core(wz, zbs, 160)
     by_core(wz, zfs, 160)
@@ -524,32 +563,39 @@
     done(wx.at[:, :, 0], xs.at[2])
     drain_halo(vd, 0)
     drain_halo(vp, 1)
-    done(n1s.at[pl.ds(0, 280)], n1ss)
-    done(n2s.at[pl.ds(0, 280)], n2ss)
-    done(s1.at[pl.ds(0, 630)], us0)
-    done(v0.at[pl.ds(0, 630)], vs0)
-
-    @pl.when(two)
-    def _():
-        done(s1.at[pl.ds(0, 350)], us1)
-        done(v1.at[pl.ds(0, 630)], vs1)
-
-    @pl.when(one)
-    def _():
-        done(s1.at[pl.ds(0, 360)], us1)
+    for i, (x0, p) in enumerate(CHUNKS):
+        done(n1s[i].at[pl.ds(0, 280)], n1ss.at[i])
+        done(n2s[i].at[pl.ds(0, 280)], n2ss.at[i])
+        done(s1.at[pl.ds(0, 63 * p)], us0.at[i])
+        done(v0.at[pl.ds(0, 63 * p)], vs0.at[i])
+
+        @pl.when(two)
+        def _(i=i, p=p):
+            done(s1.at[pl.ds(0, 35 * p)], us1.at[i])
+            done(v1.at[pl.ds(0, 63 * p)], vs1.at[i])
+
+        @pl.when(one)
+        def _(i=i, p=p):
+            done(s1.at[pl.ds(0, 36 * p)], us1.at[i])
 
     done(rb1.at[pl.ds(0, 7)], rs1)
     done(rb2.at[pl.ds(0, 63)], rs2)
+
+
+def finish(sol, res, direction, sol_out, res_out, dir_out):
+    sol_out[...] = sol[...]
+    res_out[...] = res[...]
+    dir_out[...] = direction[...]
 
 
 def per_device(sol, res, direction, prev, bx, by, bz, ex, ey, ez):
     f32 = jnp.float32
     brick = jax.ShapeDtypeStruct((CX, CY, NZ), f32)
     vmem = pl.BlockSpec(memory_space=pltpu.VMEM)
-    smem = pl.BlockSpec(memory_space=pltpu.SMEM)
     hbm = pl.BlockSpec(memory_space=pltpu.HBM)
     dma = pltpu.SemaphoreType.DMA
     shapes = [
+        (CX, CY, NZ),
         (CX, CY, NZ),
         (4, 8, 2, CX, NX),
         (NZ, NZ),
@@ -564,8 +610,9 @@
         (CX, CY, NZ),
         (400, NZ),
         (400, NZ),
-        (NZ, 400),
-        (NN, CY, 400),
+        tuple((NZ, p * CY) for _, p in CHUNKS),
+        tuple((NN, CY, p * CY) for _, p in CHUNKS),
+        (NX, NX),
         (400, NZ),
         (400, NZ),
         (1000, 128),
@@ -574,28 +621,50 @@
         (NX, 128),
         (NX, 128),
         (1000, 128),
-        (NZ, 400),
-        (NZ, 400),
+        tuple((NZ, p * CY) for _, p in CHUNKS),
+        tuple((NZ, p * CY) for _, p in CHUNKS),
         (2, 1, 128),
         (NN, 1, 128),
         (NW, 1, 128),
     ]
-    sems = [(10,), (3,), (3,), (), (8,), (), (), (), (8,), (), ()]
-    sems += [(2, 8), (2, 8), (), (8,)] + [()] * 14
-    precond, image, scal = pl.pallas_call(
+    sems = [(15,), (3,), (3,), (), (8,), (), (), (), (8,), (), ()]
+    k = len(CHUNKS)
+    sems += [(2, 8), (2, 8), (k,), (k, 8)] + [(k,)] * 10 + [()] * 4
+
+    def space(s):
+        if isinstance(s[0], tuple):
+            return [pltpu.VMEM(t, f32) for t in s]
+        return pltpu.VMEM(s, f32)
+
+    far = [
+        pltpu.with_memory_space_constraint(a, pltpu.HBM)
+        for a in (ex, ey, ez, sol, res, direction, bx, by, bz)
+    ]
+    outs = pl.pallas_call(
         kernel,
-        out_shape=(brick, brick, jax.ShapeDtypeStruct((1, 128), f32)),
-        in_specs=[smem, smem, vmem, vmem] + [hbm] * 5,
+        out_shape=(brick, brick, brick),
+        in_specs=[pl.BlockSpec(memory_space=pltpu.SMEM)] + [hbm] * 9,
         out_specs=(vmem, vmem, vmem),
-        scratch_shapes=[pltpu.VMEM(s, f32) for s in shapes] + [dma(s) for s in sems],
+        scratch_shapes=[
+            pltpu.VMEM((NX,), f32),
+            pltpu.VMEM((NZ,), f32),
+            pltpu.SMEM((NZ,), f32),
+        ]
+        + [space(s) for s in shapes]
+        + [dma(s) for s in sems],
         compiler_params=pltpu.CompilerParams(
-            collective_id=0, has_side_effects=True, vmem_limit_bytes=56 << 20
+            collective_id=0, has_side_effects=True, vmem_limit_bytes=28 << 20
         ),
         name="iterate",
-    )(ez, prev, ex, ey, res, direction, bx, by, bz)
-    ratio, alpha = scal[0, 0], scal[0, 1]
-    direction = precond + ratio * direction
-    return sol + alpha * direction, res - alpha * image, direction
+    )(prev, *far)
+    return pl.pallas_call(
+        finish,
+        out_shape=(brick, brick, brick),
+        in_specs=[vmem] * 3,
+        out_specs=(vmem, vmem, vmem),
+        compiler_params=pltpu.CompilerParams(vmem_limit_bytes=12 << 20),
+        name="finish",
+    )(*outs)
 
 
 def solution(mesh):

time: 131 us -> 117 us (0.89)
  Pallas kernels: 124 us -> 116 us
  other arithmetic: 4.1 us -> 0 us
    pallas_call x1 -> x2, Pallas kernels: 124 us -> 116 us  [the longest x1 115 us: per_device(): pl.pallas_call(kernel, out_shape=(brick, brick, brick), in_specs=[pl.Bloc...]
    add x1 -> x0, other arithmetic: 4.1 us -> none  [per_device(): return (sol + alpha * direction, res - alpha * image, direction)]
where the time goes in v3:
time: 117 us
  Pallas kernels  116 us (99%)
  between operations  1.29 us (1%)
    pallas_call x1, Pallas kernels, per_device(): pl.pallas_call(kernel, out_shape=(brick, brick, brick), in_specs=[pl.Bloc...  115 us

profile of v3, /device:TPU:1, one launch (start us, length us, event | category | flops | bytes accessed | tf_op | source)
XLA Modules:
  0.0 117.3 jit_solution(10662446655563003507)
XLA Ops:
  1.3 114.6 %iterate.1 = (f32[10,40,320]{2,1,0:T(8,128)S(1)}, f32[10,40,320]{2,1,0:T(8,128)S(1)}, f32[10,40,320]{2,1,0:T(8,128)S(1)}) custom-call(f32[1]{0:T(128)S(6)} %copy.13.prev_ref, f32[640]{0:T(1024)} %ex_hbm.1, f32[320]{0:T(512)} %ey_hbm.1, f32[320]{0:T(512)} %ez_hbm.1, f32[10,40,320]{2,1,0:T(8,128)} %sol_ref.1, f32[10,40,320]{2,1,0:T(8,128)} %res_ref.1, ...), custom_call_target="tpu_custom_call" | custom-call | tf_op jit(solution)/shard_map/iterate/pallas_call | solution.py:643
  115.9 1.3 %finish.1 = (f32[10,40,320]{2,1,0:T(8,128)}, f32[10,40,320]{2,1,0:T(8,128)}, f32[10,40,320]{2,1,0:T(8,128)}) custom-call(f32[10,40,320]{2,1,0:T(8,128)S(1)} %get-tuple-element.6.sol, f32[10,40,320]{2,1,0:T(8,128)S(1)} %get-tuple-element.7.res, f32[10,40,320]{2,1,0:T(8,128)S(1)} %get-tuple-element.8.direction), custom_call_target="tpu_custom_call" | custom-call | tf_op jit(solution)/shard_map/finish/pallas_call | solution.py:660

commit v4 on v3

--- a/solution.py
+++ b/solution.py
@@ -12,7 +12,8 @@
 MESH = pl.DeviceIdType.MESH
 NW, NN = 64, 8
 CX, CY, NZ, NX = 10, 40, 320, 640
-CHUNKS = ((0, 5), (5, 5))
+CHUNKS = ((0, 3), (3, 3), (6, 4))
+ROWS = (40, 40, 56)
 
 
 def dot(a, b, ca, cb):
@@ -25,13 +26,23 @@
     )
 
 
+def place(v):
+    return lax.div(v, 16), lax.rem(lax.div(v, 8), 2), lax.rem(v, 8)
+
+
+def device_of(v):
+    x, core, y = place(v)
+    return x * 16 + y * 2 + core
+
+
 def has_second(v):
-    return (lax.rem(v, 2) == 0) | (lax.rem(v, 16) == 1)
+    x, core, y = place(v)
+    return (core == 0) | (y == 2 * x)
 
 
 def second_tile(v):
-    odd = lax.rem(v, 2)
-    return 64 + (1 - odd) * lax.div(v, 2) + odd * (32 + lax.div(v, 16))
+    x, core, y = place(v)
+    return 64 + (1 - core) * (x * 8 + y) + core * (32 + x)
 
 
 def band(coeffs):
@@ -48,8 +59,8 @@
     return jnp.sum(jnp.sum(a * b, axis=0, keepdims=True), axis=1, keepdims=True)
 
 
-def stencil(padded, my, ky, first, second, bands, out):
-    def along_y(p, carry):
+def along_y(padded, my, ky, start, stop):
+    def step(p, carry):
         c = padded[p, 8:48, :]
         m = MASS[0] * c
         k = STIFF[0] * c
@@ -61,9 +72,11 @@
         ky[p] = k
         return carry
 
-    lax.fori_loop(0, CX + 6, along_y, 0)
-
-    def along_x(q, carry):
+    lax.fori_loop(start, stop, step, 0)
+
+
+def along_xz(my, ky, first, second, bands, out):
+    def step(q, carry):
         a = my[q + 3]
         f = MASS[0] * a
         g = STIFF[0] * a + MASS[0] * ky[q + 3]
@@ -76,10 +89,16 @@
         second[q] = f
         return carry
 
-    lax.fori_loop(0, CX, along_x, 0)
+    lax.fori_loop(0, CX, step, 0)
     g = first[...].reshape(CX * CY, NZ)
     f = second[...].reshape(CX * CY, NZ)
     out[...] = dot(g, bands[0], 1, 0) + dot(f, bands[1], 1, 0)
+
+
+def pack_plane(dst, m, rows):
+    dst[m, 40:56, 0:40] = rows[0:16, :]
+    dst[m, 40:56, 40:80] = rows[16:32, :]
+    dst[m, 40:48, 80:120] = rows[32:40, :]
 
 
 def kernel(
@@ -117,6 +136,7 @@
     n1s,
     n1r,
     wxp,
+    wide4,
     lines,
     t2,
     s1,
@@ -167,6 +187,7 @@
     core = lax.rem(w, 2)
     sibling = w + 1 - 2 * core
     gx, gy = lax.div(w, 16), lax.rem(lax.div(w, 2), 8)
+    me = gx * 16 + core * 8 + gy
     barrier = pltpu.get_barrier_semaphore()
     get_res = pltpu.make_async_copy(res_ref, res, lsem.at[8])
     get_dir = pltpu.make_async_copy(dir_ref, vd.at[pl.ds(3, CX), pl.ds(8, CY)], lsem.at[9])
@@ -261,16 +282,21 @@
 
     ownz = pltpu.make_async_copy(bz_ref, wz.at[rows_of(n)], lsem.at[0])
     owny = pltpu.make_async_copy(by_ref, wy.at[rows_of(n)], lsem.at[1])
-    ownx = pltpu.make_async_copy(bx_ref, wx.at[gx, gy, core], lsem.at[2])
+    rows_x = pl.ds(gy * CX, CX)
+    for k in range(5):
+        pltpu.make_async_copy(
+            bx_ref.at[:, pl.ds(128 * k, 128)], wx.at[k, gx, core, rows_x], lsem.at[2]
+        ).start()
     ownz.start()
     owny.start()
-    ownx.start()
     share(bz_ref, wz, zbs, zbr)
     share(by_ref, wy, ybs, ybr)
 
+    done(wx.at[:, gx, core, rows_x], lsem.at[2])
     for d in range(1, 8):
         at = {"wide": gx * 16 + lax.rem(gy + d, 8) * 2 + core}
-        send(bx_ref, wx.at[gx, gy, core], xs.at[0], xr.at[0], at)
+        block = wx.at[:, gx, core, rows_x]
+        send(block, block, xs.at[0], xr.at[0], at)
 
     has = {"xu": w < NW - 1, "xd": w > 0, "yu": n < NN - 1, "yd": n > 0}
     spans = {
@@ -280,89 +306,117 @@
     }
     rows = {
         "": (pl.ds(8, 40), pl.ds(8, 40)),
-        "yu": (pl.ds(40, 8), pl.ds(0, 8)),
-        "yd": (pl.ds(8, 8), pl.ds(48, 8)),
+        "yu": (pl.ds(45, 3), pl.ds(5, 3)),
+        "yd": (pl.ds(8, 3), pl.ds(48, 3)),
     }
     opposite = {"": "", "xu": "xd", "xd": "xu", "yu": "yd", "yd": "yu"}
-    ways = [
-        ("xu", ""),
-        ("xd", ""),
-        ("", "yu"),
-        ("", "yd"),
-        ("xu", "yu"),
-        ("xu", "yd"),
-        ("xd", "yu"),
-        ("xd", "yd"),
+    whole_way = [
+        ("xu", "", None),
+        ("xd", "", None),
+        ("xu", "yu", None),
+        ("xu", "yd", None),
+        ("xd", "yu", None),
+        ("xd", "yd", None),
+        ("", "yu", (3, 10)),
+        ("", "yd", (3, 10)),
     ]
+    ways = {"old": whole_way}
+    for i, (x0, p) in enumerate(CHUNKS):
+        side = "xd" if i == 0 else "xu" if i == len(CHUNKS) - 1 else None
+        ways[i, "x"] = [(side, b, None) for b in ("", "yu", "yd") if side]
+        ways[i, "y"] = [("", b, (3 + x0, p)) for b in ("yu", "yd")]
+    slots = {}
+    for key, items in ways.items():
+        if key != "old":
+            for item in items:
+                slots[item] = len(slots)
+
+    def slot(key, item, j):
+        return (0, j) if key == "old" else (1, slots[item])
 
     def exists(a, b):
         if a and b:
             return has[a] & has[b]
         return has[a or b]
 
-    def start_halo(v, field):
-        for i, (a, b) in enumerate(ways):
+    def side_of(a, planes, end):
+        return pl.ds(*planes) if planes else spans[a][end]
+
+    def start_halo(v, key):
+        for j, item in enumerate(ways[key]):
+            a, b, planes = item
 
             @pl.when(exists(a, b))
-            def _(i=i, a=a, b=b):
+            def _(key=key, item=item, j=j, a=a, b=b, planes=planes):
                 at = {}
                 if a:
                     at["wide"] = wup if a == "xu" else wdn
                 if b:
                     at["narrow"] = nup if b == "yu" else ndn
                 send(
-                    v.at[spans[a][0], rows[b][0]],
-                    v.at[spans[a][1], rows[b][1]],
-                    hs.at[field, i],
-                    hr.at[field, i],
+                    v.at[side_of(a, planes, 0), rows[b][0]],
+                    v.at[side_of(a, planes, 1), rows[b][1]],
+                    hs.at[slot(key, item, j)],
+                    hr.at[slot(key, item, j)],
                     at,
                 )
 
-    def wait_halo(v, field):
-        for i, (a, b) in enumerate(ways):
+    def wait_halo(v, key):
+        for j, item in enumerate(ways[key]):
+            a, b, planes = item
 
             @pl.when(exists(opposite[a], opposite[b]))
-            def _(i=i, a=a, b=b):
-                done(v.at[spans[a][1], rows[b][1]], hr.at[field, i])
-
-    def drain_halo(v, field):
-        for i, (a, b) in enumerate(ways):
+            def _(key=key, item=item, j=j, a=a, b=b, planes=planes):
+                done(v.at[side_of(a, planes, 1), rows[b][1]], hr.at[slot(key, item, j)])
+
+    def drain_halo(v, key):
+        for j, item in enumerate(ways[key]):
+            a, b, planes = item
 
             @pl.when(exists(a, b))
-            def _(i=i, a=a, b=b):
-                done(v.at[spans[a][0], rows[b][0]], hs.at[field, i])
+            def _(key=key, item=item, j=j, a=a, b=b, planes=planes):
+                done(v.at[side_of(a, planes, 0), rows[b][0]], hs.at[slot(key, item, j)])
 
     hand_over(wz, zbr, zfs, zfr)
+    done(wx.at[:, 0, 0, pl.ds(0, 70)], xr.at[0])
+    for e in range(1, 4):
+        at = {"wide": lax.rem(gx + e, 4) * 16 + gy * 2 + core}
+        send(wx.at[:, gx, core], wx.at[:, gx, core], xs.at[1], xr.at[1], at)
+
     get_res.wait()
     ownz.wait()
     by_core(wz, zfr, 120)
     for i, (x0, p) in enumerate(CHUNKS):
-        n1s[i][...] = dot(wz[...], res[x0 : x0 + p].reshape(p * CY, NZ), 0, 1)
-        pltpu.make_async_copy(n1s[i].at[rows_of(n)], n1r[i].at[n], n1rs.at[i, n]).start()
+        flat = dot(wz[...], res[x0 : x0 + p].reshape(p * CY, NZ), 0, 1)
+        n1s[i][:, 0:40, :] = flat[:, 0:120].reshape(NN, CY, 120)
+        if p == 4:
+            for m in range(NN):
+                pack_plane(n1s[i], m, flat[m * CY : m * CY + CY, 120:160])
+        pltpu.make_async_copy(n1s[i].at[n], n1r[i].at[n], n1rs.at[i, n]).start()
         for d in range(1, NN):
             v = lax.rem(n + d, NN)
             at = {"narrow": v}
-            send(n1s[i].at[rows_of(v)], n1r[i].at[n], n1ss.at[i], n1rs.at[i, n], at)
+            send(n1s[i].at[v], n1r[i].at[n], n1ss.at[i], n1rs.at[i, n], at)
 
     hand_over(wy, ybr, yfs, yfr)
     get_dir.wait()
-    start_halo(vd, 0)
-    ownx.wait()
-    done(wx.at[0, pl.ds(0, 7), 0], xr.at[0])
-    for e in range(1, 4):
-        at = {"wide": lax.rem(gx + e, 4) * 16 + gy * 2 + core}
-        send(wx.at[gx, :, core], wx.at[gx, :, core], xs.at[1], xr.at[1], at)
-
-    mine2 = second_tile(w)
-    two = has_second(w)
+    start_halo(vd, "old")
+    mine2 = second_tile(me)
+    two = has_second(me)
     one = jnp.logical_not(two)
 
     for i, (x0, p) in enumerate(CHUNKS):
         for m in range(NN):
             done(n1r[i].at[m], n1rs.at[i, m])
-            for x in range(p):
+            cols = slice(m * CY, m * CY + CY)
+            for x in range(3):
                 r = (x0 + x) * CY
-                lines[r : r + CY, m * CY : m * CY + CY] = n1r[i][m, :, x * CY : x * CY + CY]
+                lines[r : r + CY, cols] = n1r[i][m, 0:40, x * CY : x * CY + CY]
+            if p == 4:
+                r = (x0 + 3) * CY
+                lines[r : r + 16, cols] = n1r[i][m, 40:56, 0:40]
+                lines[r + 16 : r + 32, cols] = n1r[i][m, 40:56, 40:80]
+                lines[r + 32 : r + 40, cols] = n1r[i][m, 40:48, 80:120]
         if i == 0:
             owny.wait()
             by_core(wy, yfr, 120)
@@ -377,11 +431,11 @@
             s1[pl.ds(800 + x, 20, stride=10), :] = jnp.concatenate(
                 [t2[r : r + 20, 256:320], t2[r + 20 : r + CY, 256:320]], axis=1
             )
-        here = pl.ds(64 * x0 + w * p, p)
+        here = pl.ds(64 * x0 + me * p, p)
 
         def send_u(d, carry, i=i, x0=x0, p=p, here=here):
-            v = lax.rem(w + d, NW)
-            at = {"wide": v}
+            v = lax.rem(me + d, NW)
+            at = {"wide": device_of(v)}
             send(s1.at[pl.ds(v * CX + x0, p)], u0.at[here], us0.at[i], ur0.at[i], at)
 
             @pl.when(has_second(v))
@@ -392,7 +446,7 @@
             return carry
 
         lax.fori_loop(1, NW, send_u, 0, unroll=3)
-        own = pltpu.make_async_copy(s1.at[pl.ds(w * CX + x0, p)], u0.at[here], lsem.at[3])
+        own = pltpu.make_async_copy(s1.at[pl.ds(me * CX + x0, p)], u0.at[here], lsem.at[3])
         own.start()
         own.wait()
 
@@ -416,15 +470,21 @@
         low = lax.broadcasted_iota(jnp.int32, (1, 128), 1) < 64
         return row + jnp.where(low, ez_ref[n * CY + c], ez_ref[n * CY + late])
 
-    shift = jnp.concatenate([shift_row(w), shift_row(mine2)], axis=1)
-    done(wx.at[pl.ds(0, 3), :, 0], xr.at[1])
+    shift = jnp.concatenate([shift_row(me), shift_row(mine2)], axis=1)
+    done(wx.at[:, pl.ds(0, 3), 0], xr.at[1])
     send(wx.at[:, :, core], wx.at[:, :, core], xs.at[2], xr.at[2], {"wide": sibling})
-    wait_halo(vd, 0)
-    stencil(vd, my, ky, first, second, bands, image)
+    wait_halo(vd, "old")
+    along_y(vd, my, ky, 0, CX + 6)
+    along_xz(my, ky, first, second, bands, image)
 
     done(wx.at[:, :, 0], xr.at[2])
     for x0, p in CHUNKS:
-        wxp[64 * x0 : 64 * (x0 + p), :] = wx[:, :, :, x0 : x0 + p, :].reshape(64 * p, NX)
+        for x in range(p):
+            for k in range(5):
+                for g in range(8):
+                    wxp[k, pl.ds(64 * x0 + g * 8 * p + x, 8, stride=p), :] = wx[
+                        k, g // 2, g % 2, pl.ds(x0 + x, 8, stride=CX), :
+                    ]
     for i, (x0, p) in enumerate(CHUNKS):
         done(u0.at[pl.ds(0, 63 * p)], ur0.at[i])
 
@@ -433,22 +493,24 @@
             done(u1.at[pl.ds(0, 63 * p)], ur1.at[i])
 
     both = jnp.concatenate([u0[...], u1[...]], axis=1)
-    spectral = dot(wxp[...], both, 0, 0)
+    spectral = dot(jnp.concatenate([wxp[k] for k in range(5)], axis=1), both, 0, 0)
     cols = jnp.concatenate([exc[...], exc[...]], axis=1)
     spectral = spectral / (cols + shift)
     for i, (x0, p) in enumerate(CHUNKS):
         span = slice(64 * x0, 64 * (x0 + p))
-        inverse = dot(wxp[span, :], spectral, 1, 0)
+        inverse = dot(
+            jnp.concatenate([wxp[k, span, :] for k in range(5)], axis=1), spectral, 1, 0
+        )
         v0[span, :] = inverse[:, 0:128]
         v1[span, :] = inverse[:, 128:256]
-        mine = pl.ds(64 * x0 + w * p, p)
-        here = pl.ds(w * CX + x0, p)
+        mine = pl.ds(64 * x0 + me * p, p)
+        here = pl.ds(me * CX + x0, p)
         there = pl.ds(mine2 * CX + x0, p)
 
         def send_v(d, carry, i=i, x0=x0, p=p, here=here):
-            v = lax.rem(w + d, NW)
+            v = lax.rem(me + d, NW)
             src = v0.at[pl.ds(64 * x0 + v * p, p)]
-            send(src, s2.at[here], vs0.at[i], vr0.at[i], {"wide": v})
+            send(src, s2.at[here], vs0.at[i], vr0.at[i], {"wide": device_of(v)})
             return carry
 
         lax.fori_loop(1, NW, send_v, 0, unroll=3)
@@ -459,9 +521,9 @@
         @pl.when(two)
         def _(i=i, x0=x0, p=p, there=there, mine=mine):
             def send_v1(d, carry):
-                v = lax.rem(w + d, NW)
+                v = lax.rem(me + d, NW)
                 src = v1.at[pl.ds(64 * x0 + v * p, p)]
-                send(src, s2.at[there], vs1.at[i], vr1.at[i], {"wide": v})
+                send(src, s2.at[there], vs1.at[i], vr1.at[i], {"wide": device_of(v)})
                 return carry
 
             lax.fori_loop(1, NW, send_v1, 0, unroll=3)
@@ -490,26 +552,46 @@
         span = slice(x0 * CY, (x0 + p) * CY)
         lines[span, :] = dot(t2[span, :], wy[...], 1, 1)
         for m in range(NN):
-            for x in range(p):
+            cols = slice(m * CY, m * CY + CY)
+            for x in range(3):
                 r = (x0 + x) * CY
-                n2s[i][m * CY : m * CY + CY, x * CY : x * CY + CY] = lines[
-                    r : r + CY, m * CY : m * CY + CY
-                ]
-        own = pltpu.make_async_copy(n2s[i].at[rows_of(n)], n2r[i].at[rows_of(n)], lsem.at[7])
+                n2s[i][m, 0:40, x * CY : x * CY + CY] = lines[r : r + CY, cols]
+            if p == 4:
+                r = (x0 + 3) * CY
+                pack_plane(n2s[i], m, lines[r : r + CY, cols])
+        own = pltpu.make_async_copy(n2s[i].at[n], n2r[i].at[n], lsem.at[7])
         own.start()
         for d in range(1, NN):
             v = lax.rem(n + d, NN)
-            at = {"narrow": v}
-            send(n2s[i].at[rows_of(v)], n2r[i].at[rows_of(n)], n2ss.at[i], n2rs.at[i], at)
+            send(n2s[i].at[v], n2r[i].at[n], n2ss.at[i], n2rs.at[i], {"narrow": v})
         own.wait()
 
     for i, (x0, p) in enumerate(CHUNKS):
-        done(n2r[i].at[pl.ds(0, 280)], n2rs.at[i])
-        piece = dot(n2r[i][...], wz[...], 0, 1).reshape(p, CY, NZ)
-        vp[3 + x0 : 3 + x0 + p, 8:48, :] = piece
-    start_halo(vp, 1)
-    wait_halo(vp, 1)
-    stencil(vp, my, ky, first, second, bands, fresh)
+        done(n2r[i].at[pl.ds(0, 7)], n2rs.at[i])
+        flat = n2r[i][:, 0:40, :].reshape(NZ, 120)
+        if p == 4:
+            wide4[:, 0:120] = flat
+            for m in range(NN):
+                r = m * CY
+                wide4[r : r + 16, 120:160] = n2r[i][m, 40:56, 0:40]
+                wide4[r + 16 : r + 32, 120:160] = n2r[i][m, 40:56, 40:80]
+                wide4[r + 32 : r + 40, 120:160] = n2r[i][m, 40:48, 80:120]
+            flat = wide4[...]
+        vp[3 + x0 : 3 + x0 + p, 8:48, :] = dot(flat, wz[...], 0, 1).reshape(p, CY, NZ)
+        start_halo(vp, (i, "x"))
+        start_halo(vp, (i, "y"))
+        if i > 0:
+            q0, q = CHUNKS[i - 1]
+            wait_halo(vp, (i - 1, "y"))
+            along_y(vp, my, ky, 3 + q0, 3 + q0 + q)
+    last = len(CHUNKS) - 1
+    wait_halo(vp, (last, "y"))
+    along_y(vp, my, ky, 3 + CHUNKS[last][0], 3 + CX)
+    wait_halo(vp, (last, "x"))
+    along_y(vp, my, ky, 0, 3)
+    wait_halo(vp, (0, "x"))
+    along_y(vp, my, ky, CX + 3, CX + 6)
+    along_xz(my, ky, first, second, bands, fresh)
 
     precond = vp[3:13, 8:48, :].reshape(CX * CY, NZ)
     direction = vd[3:13, 8:48, :].reshape(CX * CY, NZ)
@@ -558,14 +640,16 @@
     by_core(wz, zfs, 160)
     by_core(wy, ybs, 160)
     by_core(wy, yfs, 160)
-    done(wx.at[0, pl.ds(0, 7), 0], xs.at[0])
-    done(wx.at[pl.ds(0, 3), :, 0], xs.at[1])
+    done(wx.at[:, 0, 0, pl.ds(0, 70)], xs.at[0])
+    done(wx.at[:, pl.ds(0, 3), 0], xs.at[1])
     done(wx.at[:, :, 0], xs.at[2])
-    drain_halo(vd, 0)
-    drain_halo(vp, 1)
+    drain_halo(vd, "old")
+    for i in range(len(CHUNKS)):
+        drain_halo(vp, (i, "x"))
+        drain_halo(vp, (i, "y"))
     for i, (x0, p) in enumerate(CHUNKS):
-        done(n1s[i].at[pl.ds(0, 280)], n1ss.at[i])
-        done(n2s[i].at[pl.ds(0, 280)], n2ss.at[i])
+        done(n1s[i].at[pl.ds(0, 7)], n1ss.at[i])
+        done(n2s[i].at[pl.ds(0, 7)], n2ss.at[i])
         done(s1.at[pl.ds(0, 63 * p)], us0.at[i])
         done(v0.at[pl.ds(0, 63 * p)], vs0.at[i])
 
@@ -597,7 +681,7 @@
     shapes = [
         (CX, CY, NZ),
         (CX, CY, NZ),
-        (4, 8, 2, CX, NX),
+        (5, 4, 2, 80, 128),
         (NZ, NZ),
         (NZ, NZ),
         (2, NZ, NZ),
@@ -610,9 +694,10 @@
         (CX, CY, NZ),
         (400, NZ),
         (400, NZ),
-        tuple((NZ, p * CY) for _, p in CHUNKS),
-        tuple((NN, CY, p * CY) for _, p in CHUNKS),
-        (NX, NX),
+        tuple((NN, r, 120) for r in ROWS),
+        tuple((NN, r, 120) for r in ROWS),
+        (5, NX, 128),
+        (NZ, 160),
         (400, NZ),
         (400, NZ),
         (1000, 128),
@@ -621,15 +706,15 @@
         (NX, 128),
         (NX, 128),
         (1000, 128),
-        tuple((NZ, p * CY) for _, p in CHUNKS),
-        tuple((NZ, p * CY) for _, p in CHUNKS),
+        tuple((NN, r, 120) for r in ROWS),
+        tuple((NN, r, 120) for r in ROWS),
         (2, 1, 128),
         (NN, 1, 128),
         (NW, 1, 128),
     ]
     sems = [(15,), (3,), (3,), (), (8,), (), (), (), (8,), (), ()]
     k = len(CHUNKS)
-    sems += [(2, 8), (2, 8), (k,), (k, 8)] + [(k,)] * 10 + [()] * 4
+    sems += [(2, 12), (2, 12), (k,), (k, 8)] + [(k,)] * 10 + [()] * 4
 
     def space(s):
         if isinstance(s[0], tuple):

time: 117 us -> 106 us (0.906)
  Pallas kernels: 116 us -> 104 us
    pallas_call x1, Pallas kernels: 115 us -> 103 us  [per_device(): pl.pallas_call(kernel, out_shape=(brick, brick, brick), in_specs=[pl.Bloc...]
where the time goes in v4:
time: 106 us; the launch traced here: 105 us
  Pallas kernels  104 us (98%)
  between operations  1.29 us (1%)
    pallas_call x1, Pallas kernels, per_device(): pl.pallas_call(kernel, out_shape=(brick, brick, brick), in_specs=[pl.Bloc...  103 us

profile of v4, /device:TPU:1, one launch (start us, length us, event | category | flops | bytes accessed | tf_op | source)
XLA Modules:
  0.0 105.5 jit_solution(8841422873938784049)
XLA Ops:
  1.3 102.8 %iterate.1 = (f32[10,40,320]{2,1,0:T(8,128)S(1)}, f32[10,40,320]{2,1,0:T(8,128)S(1)}, f32[10,40,320]{2,1,0:T(8,128)S(1)}) custom-call(f32[1]{0:T(128)S(6)} %copy.13.prev_ref, f32[640]{0:T(1024)} %ex_hbm.1, f32[320]{0:T(512)} %ey_hbm.1, f32[320]{0:T(512)} %ez_hbm.1, f32[10,40,320]{2,1,0:T(8,128)} %sol_ref.1, f32[10,40,320]{2,1,0:T(8,128)} %res_ref.1, ...), custom_call_target="tpu_custom_call" | custom-call | tf_op jit(solution)/shard_map/iterate/pallas_call | solution.py:728
  104.1 1.3 %finish.1 = (f32[10,40,320]{2,1,0:T(8,128)}, f32[10,40,320]{2,1,0:T(8,128)}, f32[10,40,320]{2,1,0:T(8,128)}) custom-call(f32[10,40,320]{2,1,0:T(8,128)S(1)} %get-tuple-element.6.sol, f32[10,40,320]{2,1,0:T(8,128)S(1)} %get-tuple-element.7.res, f32[10,40,320]{2,1,0:T(8,128)S(1)} %get-tuple-element.8.direction), custom_call_target="tpu_custom_call" | custom-call | tf_op jit(solution)/shard_map/finish/pallas_call | solution.py:745

commit v5 on v4

--- a/solution.py
+++ b/solution.py
@@ -30,6 +30,24 @@
     return lax.div(v, 16), lax.rem(lax.div(v, 8), 2), lax.rem(v, 8)
 
 
+def split(x):
+    high = x.astype(jnp.bfloat16)
+    return high, (x - high.astype(jnp.float32)).astype(jnp.bfloat16)
+
+
+def dot3(a, b, ca, cb):
+    def one(x, y):
+        return lax.dot_general(
+            x, y, (((ca,), (cb,)), ((), ())), preferred_element_type=jnp.float32
+        )
+
+    return one(a[0], b[0]) + one(a[0], b[1]) + one(a[1], b[0])
+
+
+def keep(ref, x):
+    ref[0], ref[1] = split(x)
+
+
 def device_of(v):
     x, core, y = place(v)
     return x * 16 + y * 2 + core
@@ -40,9 +58,10 @@
     return (core == 0) | (y == 2 * x)
 
 
-def second_tile(v):
+def first_tile(v):
     x, core, y = place(v)
-    return 64 + (1 - core) * (x * 8 + y) + core * (32 + x)
+    q = x * 8 + y
+    return (1 - core) * 2 * q + core * (64 + q + lax.div(q + 9, 10))
 
 
 def band(coeffs):
@@ -90,9 +109,10 @@
         return carry
 
     lax.fori_loop(0, CX, step, 0)
-    g = first[...].reshape(CX * CY, NZ)
-    f = second[...].reshape(CX * CY, NZ)
-    out[...] = dot(g, bands[0], 1, 0) + dot(f, bands[1], 1, 0)
+    g = split(first[...].reshape(CX * CY, NZ))
+    f = split(second[...].reshape(CX * CY, NZ))
+    m, k = ((bands[i, 0], bands[i, 1]) for i in range(2))
+    out[...] = dot3(g, m, 1, 0) + dot3(f, k, 1, 0)
 
 
 def pack_plane(dst, m, rows):
@@ -137,13 +157,16 @@
     n1r,
     wxp,
     wide4,
+    wxr,
+    wxc,
+    wyr,
+    wyc,
+    wzc,
     lines,
     t2,
     s1,
-    u0,
-    u1,
-    v0,
-    v1,
+    ub,
+    vb,
     s2,
     n2s,
     n2r,
@@ -165,14 +188,10 @@
     hr,
     n1ss,
     n1rs,
-    us0,
-    us1,
-    ur0,
-    ur1,
-    vs0,
-    vs1,
-    vr0,
-    vr1,
+    us,
+    ur,
+    vs,
+    vr,
     n2ss,
     n2rs,
     rs1,
@@ -207,7 +226,7 @@
         for p in range(3, 13):
             v[p, 0:8, :] = jnp.zeros((8, NZ), jnp.float32)
             v[p, 48:56, :] = jnp.zeros((8, NZ), jnp.float32)
-    u1[...] = jnp.zeros_like(u1)
+    ub[...] = jnp.zeros_like(ub)
 
     def greet(d, carry):
         pl.semaphore_signal(
@@ -226,8 +245,8 @@
                 barrier, inc=1, device_id={"wide": a, "narrow": b}, device_id_type=MESH
             )
 
-    bands[0] = band(MASS)
-    bands[1] = band(STIFF)
+    keep(bands.at[0], band(MASS))
+    keep(bands.at[1], band(STIFF))
     for c in small:
         c.wait()
     exc[...] = jnp.transpose(jnp.broadcast_to(ex_ref[...].reshape(1, NX), (128, NX)))
@@ -401,9 +420,13 @@
     hand_over(wy, ybr, yfs, yfr)
     get_dir.wait()
     start_halo(vd, "old")
-    mine2 = second_tile(me)
+    tile = first_tile(me)
     two = has_second(me)
     one = jnp.logical_not(two)
+
+    owny.wait()
+    by_core(wy, yfr, 120)
+    keep(wyr, wy[...])
 
     for i, (x0, p) in enumerate(CHUNKS):
         for m in range(NN):
@@ -417,46 +440,53 @@
                 lines[r : r + 16, cols] = n1r[i][m, 40:56, 0:40]
                 lines[r + 16 : r + 32, cols] = n1r[i][m, 40:56, 40:80]
                 lines[r + 32 : r + 40, cols] = n1r[i][m, 40:48, 80:120]
-        if i == 0:
-            owny.wait()
-            by_core(wy, yfr, 120)
         span = slice(x0 * CY, (x0 + p) * CY)
-        t2[span, :] = dot(lines[span, :], wy[...], 1, 0)
-        for x in range(x0, x0 + p):
-            r = x * CY
+        t2[span, :] = dot3(split(lines[span, :]), (wyr[0], wyr[1]), 1, 0)
+        for x in range(p):
+            r = (x0 + x) * CY
+            at = 100 * x0 + x
             for j in range(2):
-                s1[pl.ds(j * 400 + x, 40, stride=10), :] = t2[
+                s1[pl.ds(at + j * 40 * p, 40, stride=p), :] = t2[
                     r : r + CY, 128 * j : 128 * j + 128
                 ]
-            s1[pl.ds(800 + x, 20, stride=10), :] = jnp.concatenate(
+            s1[pl.ds(at + 80 * p, 20, stride=p), :] = jnp.concatenate(
                 [t2[r : r + 20, 256:320], t2[r + 20 : r + CY, 256:320]], axis=1
             )
-        here = pl.ds(64 * x0 + me * p, p)
-
-        def send_u(d, carry, i=i, x0=x0, p=p, here=here):
+
+        def send_u(d, carry, i=i, x0=x0, p=p):
             v = lax.rem(me + d, NW)
             at = {"wide": device_of(v)}
-            send(s1.at[pl.ds(v * CX + x0, p)], u0.at[here], us0.at[i], ur0.at[i], at)
-
-            @pl.when(has_second(v))
+            src, dst = 100 * x0 + first_tile(v) * p, 128 * x0 + me * 2 * p
+            double = has_second(v)
+
+            @pl.when(double)
             def _():
-                src = s1.at[pl.ds(second_tile(v) * CX + x0, p)]
-                send(src, u1.at[here], us1.at[i], ur1.at[i], at)
+                send(s1.at[pl.ds(src, 2 * p)], ub.at[pl.ds(dst, 2 * p)], us.at[i], ur.at[i], at)
+
+            @pl.when(jnp.logical_not(double))
+            def _():
+                send(s1.at[pl.ds(src, p)], ub.at[pl.ds(dst, p)], us.at[i], ur.at[i], at)
 
             return carry
 
         lax.fori_loop(1, NW, send_u, 0, unroll=3)
-        own = pltpu.make_async_copy(s1.at[pl.ds(me * CX + x0, p)], u0.at[here], lsem.at[3])
-        own.start()
-        own.wait()
-
-        @pl.when(two)
-        def _(x0=x0, p=p, here=here):
+
+        def keep_u(size, x0=x0, p=p):
             c = pltpu.make_async_copy(
-                s1.at[pl.ds(mine2 * CX + x0, p)], u1.at[here], lsem.at[4]
+                s1.at[pl.ds(100 * x0 + tile * p, size)],
+                ub.at[pl.ds(128 * x0 + me * 2 * p, size)],
+                lsem.at[3],
             )
             c.start()
             c.wait()
+
+        @pl.when(two)
+        def _(p=p, keep_u=keep_u):
+            keep_u(2 * p)
+
+        @pl.when(one)
+        def _(p=p, keep_u=keep_u):
+            keep_u(p)
 
     ey = ey_ref[...].reshape(1, NZ)
 
@@ -470,7 +500,7 @@
         low = lax.broadcasted_iota(jnp.int32, (1, 128), 1) < 64
         return row + jnp.where(low, ez_ref[n * CY + c], ez_ref[n * CY + late])
 
-    shift = jnp.concatenate([shift_row(me), shift_row(mine2)], axis=1)
+    shift = jnp.concatenate([shift_row(tile), shift_row(jnp.minimum(tile + 1, 99))], axis=1)
     done(wx.at[:, pl.ds(0, 3), 0], xr.at[1])
     send(wx.at[:, :, core], wx.at[:, :, core], xs.at[2], xr.at[2], {"wide": sibling})
     wait_halo(vd, "old")
@@ -478,79 +508,98 @@
     along_xz(my, ky, first, second, bands, image)
 
     done(wx.at[:, :, 0], xr.at[2])
-    for x0, p in CHUNKS:
-        for x in range(p):
-            for k in range(5):
-                for g in range(8):
-                    wxp[k, pl.ds(64 * x0 + g * 8 * p + x, 8, stride=p), :] = wx[
-                        k, g // 2, g % 2, pl.ds(x0 + x, 8, stride=CX), :
-                    ]
+    for k in range(5):
+        for x in range(CX):
+            for g in range(8):
+                wxp[k, x * 64 + g * 8 : x * 64 + g * 8 + 8, :] = wx[
+                    k, g // 2, g % 2, pl.ds(x, 8, stride=CX), :
+                ]
+        cols = slice(128 * k, 128 * k + 128)
+        wxr[0, :, cols], wxr[1, :, cols] = split(wxp[k])
+        wxc[0, cols, :], wxc[1, cols, :] = split(jnp.transpose(wxp[k]))
+    keep(wyc, jnp.transpose(wy[...]))
+    keep(wzc, jnp.transpose(wz[...]))
     for i, (x0, p) in enumerate(CHUNKS):
-        done(u0.at[pl.ds(0, 63 * p)], ur0.at[i])
 
         @pl.when(two)
         def _(i=i, p=p):
-            done(u1.at[pl.ds(0, 63 * p)], ur1.at[i])
-
-    both = jnp.concatenate([u0[...], u1[...]], axis=1)
-    spectral = dot(jnp.concatenate([wxp[k] for k in range(5)], axis=1), both, 0, 0)
+            done(ub.at[pl.ds(0, 126 * p)], ur.at[i])
+
+        @pl.when(one)
+        def _(i=i, p=p):
+            done(ub.at[pl.ds(0, 63 * p)], ur.at[i])
+
+    both = jnp.concatenate(
+        [
+            jnp.concatenate(
+                [
+                    ub[pl.ds(128 * x0 + k * p + x, 64, stride=2 * p), :]
+                    for x0, p in CHUNKS
+                    for x in range(p)
+                ],
+                axis=0,
+            )
+            for k in range(2)
+        ],
+        axis=1,
+    )
+    spectral = dot3((wxc[0], wxc[1]), split(both), 1, 0)
     cols = jnp.concatenate([exc[...], exc[...]], axis=1)
-    spectral = spectral / (cols + shift)
+    spectral = split(spectral / (cols + shift))
     for i, (x0, p) in enumerate(CHUNKS):
         span = slice(64 * x0, 64 * (x0 + p))
-        inverse = dot(
-            jnp.concatenate([wxp[k, span, :] for k in range(5)], axis=1), spectral, 1, 0
-        )
-        v0[span, :] = inverse[:, 0:128]
-        v1[span, :] = inverse[:, 128:256]
-        mine = pl.ds(64 * x0 + me * p, p)
-        here = pl.ds(me * CX + x0, p)
-        there = pl.ds(mine2 * CX + x0, p)
-
-        def send_v(d, carry, i=i, x0=x0, p=p, here=here):
-            v = lax.rem(me + d, NW)
-            src = v0.at[pl.ds(64 * x0 + v * p, p)]
-            send(src, s2.at[here], vs0.at[i], vr0.at[i], {"wide": device_of(v)})
-            return carry
-
-        lax.fori_loop(1, NW, send_v, 0, unroll=3)
-        own = pltpu.make_async_copy(v0.at[mine], s2.at[here], lsem.at[5])
-        own.start()
-        own.wait()
-
-        @pl.when(two)
-        def _(i=i, x0=x0, p=p, there=there, mine=mine):
-            def send_v1(d, carry):
+        inverse = dot3((wxr[0, span, :], wxr[1, span, :]), spectral, 1, 0)
+        for x in range(p):
+            for k in range(2):
+                vb[pl.ds(128 * x0 + k * p + x, 64, stride=2 * p), :] = inverse[
+                    x * 64 : x * 64 + 64, 128 * k : 128 * k + 128
+                ]
+
+        def back(size, i=i, x0=x0, p=p):
+            here = pl.ds(100 * x0 + tile * p, size)
+
+            def send_v(d, carry):
                 v = lax.rem(me + d, NW)
-                src = v1.at[pl.ds(64 * x0 + v * p, p)]
-                send(src, s2.at[there], vs1.at[i], vr1.at[i], {"wide": device_of(v)})
+                src = vb.at[pl.ds(128 * x0 + v * 2 * p, size)]
+                send(src, s2.at[here], vs.at[i], vr.at[i], {"wide": device_of(v)})
                 return carry
 
-            lax.fori_loop(1, NW, send_v1, 0, unroll=3)
-            c = pltpu.make_async_copy(v1.at[mine], s2.at[there], lsem.at[6])
+            lax.fori_loop(1, NW, send_v, 0, unroll=3)
+            c = pltpu.make_async_copy(
+                vb.at[pl.ds(128 * x0 + me * 2 * p, size)], s2.at[here], lsem.at[5]
+            )
             c.start()
             c.wait()
 
+        @pl.when(two)
+        def _(p=p, back=back):
+            back(2 * p)
+
+        @pl.when(one)
+        def _(p=p, back=back):
+            back(p)
+
     for i, (x0, p) in enumerate(CHUNKS):
-        done(s2.at[pl.ds(0, 63 * p)], vr0.at[i])
-
         @pl.when(two)
         def _(i=i, p=p):
-            done(s2.at[pl.ds(0, 35 * p)], vr1.at[i])
+            done(s2.at[pl.ds(0, 98 * p)], vr.at[i])
 
         @pl.when(one)
         def _(i=i, p=p):
-            done(s2.at[pl.ds(0, 36 * p)], vr1.at[i])
-
-        for x in range(x0, x0 + p):
-            r = x * CY
+            done(s2.at[pl.ds(0, 99 * p)], vr.at[i])
+
+        for x in range(p):
+            r = (x0 + x) * CY
+            at = 100 * x0 + x
             for j in range(2):
-                t2[r : r + CY, 128 * j : 128 * j + 128] = s2[pl.ds(j * 400 + x, 40, stride=10), :]
-            b = s2[pl.ds(800 + x, 20, stride=10), :]
+                t2[r : r + CY, 128 * j : 128 * j + 128] = s2[
+                    pl.ds(at + j * 40 * p, 40, stride=p), :
+                ]
+            b = s2[pl.ds(at + 80 * p, 20, stride=p), :]
             t2[r : r + 20, 256:320] = b[:, 0:64]
             t2[r + 20 : r + CY, 256:320] = b[:, 64:128]
         span = slice(x0 * CY, (x0 + p) * CY)
-        lines[span, :] = dot(t2[span, :], wy[...], 1, 1)
+        lines[span, :] = dot3(split(t2[span, :]), (wyc[0], wyc[1]), 1, 0)
         for m in range(NN):
             cols = slice(m * CY, m * CY + CY)
             for x in range(3):
@@ -577,7 +626,9 @@
                 wide4[r + 16 : r + 32, 120:160] = n2r[i][m, 40:56, 40:80]
                 wide4[r + 32 : r + 40, 120:160] = n2r[i][m, 40:48, 80:120]
             flat = wide4[...]
-        vp[3 + x0 : 3 + x0 + p, 8:48, :] = dot(flat, wz[...], 0, 1).reshape(p, CY, NZ)
+        vp[3 + x0 : 3 + x0 + p, 8:48, :] = dot3(
+            split(jnp.transpose(flat)), (wzc[0], wzc[1]), 1, 0
+        ).reshape(p, CY, NZ)
         start_halo(vp, (i, "x"))
         start_halo(vp, (i, "y"))
         if i > 0:
@@ -650,17 +701,16 @@
     for i, (x0, p) in enumerate(CHUNKS):
         done(n1s[i].at[pl.ds(0, 7)], n1ss.at[i])
         done(n2s[i].at[pl.ds(0, 7)], n2ss.at[i])
-        done(s1.at[pl.ds(0, 63 * p)], us0.at[i])
-        done(v0.at[pl.ds(0, 63 * p)], vs0.at[i])
 
         @pl.when(two)
         def _(i=i, p=p):
-            done(s1.at[pl.ds(0, 35 * p)], us1.at[i])
-            done(v1.at[pl.ds(0, 63 * p)], vs1.at[i])
+            done(s1.at[pl.ds(0, 98 * p)], us.at[i])
+            done(vb.at[pl.ds(0, 126 * p)], vs.at[i])
 
         @pl.when(one)
         def _(i=i, p=p):
-            done(s1.at[pl.ds(0, 36 * p)], us1.at[i])
+            done(s1.at[pl.ds(0, 99 * p)], us.at[i])
+            done(vb.at[pl.ds(0, 63 * p)], vs.at[i])
 
     done(rb1.at[pl.ds(0, 7)], rs1)
     done(rb2.at[pl.ds(0, 63)], rs2)
@@ -684,7 +734,7 @@
         (5, 4, 2, 80, 128),
         (NZ, NZ),
         (NZ, NZ),
-        (2, NZ, NZ),
+        [2, 2, NZ, NZ],
         (NX, 128),
         (16, 56, NZ),
         (16, 56, NZ),
@@ -698,13 +748,16 @@
         tuple((NN, r, 120) for r in ROWS),
         (5, NX, 128),
         (NZ, 160),
+        [2, NX, NX],
+        [2, NX, NX],
+        [2, NZ, NZ],
+        [2, NZ, NZ],
+        [2, NZ, NZ],
         (400, NZ),
         (400, NZ),
         (1000, 128),
-        (NX, 128),
-        (NX, 128),
-        (NX, 128),
-        (NX, 128),
+        (2 * NX, 128),
+        (2 * NX, 128),
         (1000, 128),
         tuple((NN, r, 120) for r in ROWS),
         tuple((NN, r, 120) for r in ROWS),
@@ -714,12 +767,12 @@
     ]
     sems = [(15,), (3,), (3,), (), (8,), (), (), (), (8,), (), ()]
     k = len(CHUNKS)
-    sems += [(2, 12), (2, 12), (k,), (k, 8)] + [(k,)] * 10 + [()] * 4
+    sems += [(2, 12), (2, 12), (k,), (k, 8)] + [(k,)] * 6 + [()] * 4
 
     def space(s):
         if isinstance(s[0], tuple):
             return [pltpu.VMEM(t, f32) for t in s]
-        return pltpu.VMEM(s, f32)
+        return pltpu.VMEM(tuple(s), jnp.bfloat16 if isinstance(s, list) else f32)
 
     far = [
         pltpu.with_memory_space_constraint(a, pltpu.HBM)

time: 106 us -> 105 us (level)
  no operation moved by 1% of the time
where the time goes in v5:
time: 105 us
  Pallas kernels  104 us (99%)
  between operations  1.29 us (1%)
    pallas_call x1, Pallas kernels, per_device(): pl.pallas_call(kernel, out_shape=(brick, brick, brick), in_specs=[pl.Bloc...  103 us

profile of v5, /device:TPU:1, one launch (start us, length us, event | category | flops | bytes accessed | tf_op | source)
XLA Modules:
  0.0 105.2 jit_solution(16866478135698745151)
XLA Ops:
  1.3 102.6 %iterate.1 = (f32[10,40,320]{2,1,0:T(8,128)S(1)}, f32[10,40,320]{2,1,0:T(8,128)S(1)}, f32[10,40,320]{2,1,0:T(8,128)S(1)}) custom-call(f32[1]{0:T(128)S(6)} %copy.13.prev_ref, f32[640]{0:T(1024)} %ex_hbm.1, f32[320]{0:T(512)} %ey_hbm.1, f32[320]{0:T(512)} %ez_hbm.1, f32[10,40,320]{2,1,0:T(8,128)} %sol_ref.1, f32[10,40,320]{2,1,0:T(8,128)} %res_ref.1, ...), custom_call_target="tpu_custom_call" | custom-call | tf_op jit(solution)/shard_map/iterate/pallas_call | solution.py:781
  103.9 1.3 %finish.1 = (f32[10,40,320]{2,1,0:T(8,128)}, f32[10,40,320]{2,1,0:T(8,128)}, f32[10,40,320]{2,1,0:T(8,128)}) custom-call(f32[10,40,320]{2,1,0:T(8,128)S(1)} %get-tuple-element.6.sol, f32[10,40,320]{2,1,0:T(8,128)S(1)} %get-tuple-element.7.res, f32[10,40,320]{2,1,0:T(8,128)S(1)} %get-tuple-element.8.direction), custom_call_target="tpu_custom_call" | custom-call | tf_op jit(solution)/shard_map/finish/pallas_call | solution.py:798

commit v6 on v5

--- a/solution.py
+++ b/solution.py
@@ -12,8 +12,9 @@
 MESH = pl.DeviceIdType.MESH
 NW, NN = 64, 8
 CX, CY, NZ, NX = 10, 40, 320, 640
-CHUNKS = ((0, 3), (3, 3), (6, 4))
-ROWS = (40, 40, 56)
+CHUNKS = ((0, 3), (6, 4), (3, 3))
+ROWS = (40, 56, 40)
+FAR = (4, 3, 5, 2, 6, 1, 7)
 
 
 def dot(a, b, ca, cb):
@@ -26,10 +27,6 @@
     )
 
 
-def place(v):
-    return lax.div(v, 16), lax.rem(lax.div(v, 8), 2), lax.rem(v, 8)
-
-
 def split(x):
     high = x.astype(jnp.bfloat16)
     return high, (x - high.astype(jnp.float32)).astype(jnp.bfloat16)
@@ -48,20 +45,13 @@
     ref[0], ref[1] = split(x)
 
 
-def device_of(v):
-    x, core, y = place(v)
-    return x * 16 + y * 2 + core
-
-
-def has_second(v):
-    x, core, y = place(v)
+def has_second(x, core, y):
     return (core == 0) | (y == 2 * x)
 
 
-def first_tile(v):
-    x, core, y = place(v)
+def first_tile(x, core, y):
     q = x * 8 + y
-    return (1 - core) * 2 * q + core * (64 + q + lax.div(q + 9, 10))
+    return (1 - core) * 2 * q + core * (64 + q + x + jnp.where(y > 2 * x, 1, 0))
 
 
 def band(coeffs):
@@ -208,6 +198,26 @@
     gx, gy = lax.div(w, 16), lax.rem(lax.div(w, 2), 8)
     me = gx * 16 + core * 8 + gy
     barrier = pltpu.get_barrier_semaphore()
+    lines_x = [lax.rem(gx + e, 4) for e in range(4)]
+    cores = [core, 1 - core]
+
+    def each_wide(fn):
+        def ring(k, carry):
+            y = lax.rem(gy + 4 + lax.div(k + 1, 2) * (1 - 2 * lax.rem(k, 2)), 8)
+            for e in (2, 1, 3, 0):
+                for c in (1, 0):
+                    fn(lines_x[e], cores[c], y)
+            return carry
+
+        lax.fori_loop(0, 7, ring, 0)
+        for e in (2, 1, 3, 0):
+            for c in (1, 0):
+                if e or c:
+                    fn(lines_x[e], cores[c], gy)
+
+    def device(x, c, y):
+        return {"wide": x * 16 + y * 2 + c}
+
     get_res = pltpu.make_async_copy(res_ref, res, lsem.at[8])
     get_dir = pltpu.make_async_copy(dir_ref, vd.at[pl.ds(3, CX), pl.ds(8, CY)], lsem.at[9])
     get_sol = pltpu.make_async_copy(sol_ref, sol, lsem.at[10])
@@ -228,14 +238,11 @@
             v[p, 48:56, :] = jnp.zeros((8, NZ), jnp.float32)
     ub[...] = jnp.zeros_like(ub)
 
-    def greet(d, carry):
-        pl.semaphore_signal(
-            barrier, inc=1, device_id={"wide": lax.rem(w + d, NW)}, device_id_type=MESH
-        )
-        return carry
-
-    lax.fori_loop(1, NW, greet, 0)
-    for d in range(1, NN):
+    def greet(x, c, y):
+        pl.semaphore_signal(barrier, inc=1, device_id=device(x, c, y), device_id_type=MESH)
+
+    each_wide(greet)
+    for d in FAR:
         pl.semaphore_signal(
             barrier, inc=1, device_id={"narrow": lax.rem(n + d, NN)}, device_id_type=MESH
         )
@@ -274,7 +281,7 @@
         return pl.ds(pl.multiple_of(v * CY, 8), CY)
 
     def share(own, whole, ssem, rsem):
-        for d in range(1, NN):
+        for d in FAR:
 
             @pl.when(near(d))
             def _(d=d):
@@ -282,7 +289,7 @@
                 send(own, whole.at[rows_of(n)], ssem, rsem.at[d], at)
 
     def hand_over(whole, rsem, fsem, gsem):
-        for d in range(1, NN):
+        for d in FAR:
 
             @pl.when(near(d))
             def _(d=d):
@@ -312,7 +319,7 @@
     share(by_ref, wy, ybs, ybr)
 
     done(wx.at[:, gx, core, rows_x], lsem.at[2])
-    for d in range(1, 8):
+    for d in FAR:
         at = {"wide": gx * 16 + lax.rem(gy + d, 8) * 2 + core}
         block = wx.at[:, gx, core, rows_x]
         send(block, block, xs.at[0], xr.at[0], at)
@@ -341,7 +348,7 @@
     ]
     ways = {"old": whole_way}
     for i, (x0, p) in enumerate(CHUNKS):
-        side = "xd" if i == 0 else "xu" if i == len(CHUNKS) - 1 else None
+        side = ("xd", "xu", None)[i]
         ways[i, "x"] = [(side, b, None) for b in ("", "yu", "yd") if side]
         ways[i, "y"] = [("", b, (3 + x0, p)) for b in ("yu", "yd")]
     slots = {}
@@ -398,7 +405,7 @@
 
     hand_over(wz, zbr, zfs, zfr)
     done(wx.at[:, 0, 0, pl.ds(0, 70)], xr.at[0])
-    for e in range(1, 4):
+    for e in (2, 1, 3):
         at = {"wide": lax.rem(gx + e, 4) * 16 + gy * 2 + core}
         send(wx.at[:, gx, core], wx.at[:, gx, core], xs.at[1], xr.at[1], at)
 
@@ -412,7 +419,7 @@
             for m in range(NN):
                 pack_plane(n1s[i], m, flat[m * CY : m * CY + CY, 120:160])
         pltpu.make_async_copy(n1s[i].at[n], n1r[i].at[n], n1rs.at[i, n]).start()
-        for d in range(1, NN):
+        for d in FAR:
             v = lax.rem(n + d, NN)
             at = {"narrow": v}
             send(n1s[i].at[v], n1r[i].at[n], n1ss.at[i], n1rs.at[i, n], at)
@@ -420,8 +427,8 @@
     hand_over(wy, ybr, yfs, yfr)
     get_dir.wait()
     start_halo(vd, "old")
-    tile = first_tile(me)
-    two = has_second(me)
+    tile = first_tile(gx, core, gy)
+    two = has_second(gx, core, gy)
     one = jnp.logical_not(two)
 
     owny.wait()
@@ -453,11 +460,10 @@
                 [t2[r : r + 20, 256:320], t2[r + 20 : r + CY, 256:320]], axis=1
             )
 
-        def send_u(d, carry, i=i, x0=x0, p=p):
-            v = lax.rem(me + d, NW)
-            at = {"wide": device_of(v)}
-            src, dst = 100 * x0 + first_tile(v) * p, 128 * x0 + me * 2 * p
-            double = has_second(v)
+        def send_u(x, c, y, i=i, x0=x0, p=p):
+            at = device(x, c, y)
+            src, dst = 100 * x0 + first_tile(x, c, y) * p, 128 * x0 + me * 2 * p
+            double = has_second(x, c, y)
 
             @pl.when(double)
             def _():
@@ -467,9 +473,7 @@
             def _():
                 send(s1.at[pl.ds(src, p)], ub.at[pl.ds(dst, p)], us.at[i], ur.at[i], at)
 
-            return carry
-
-        lax.fori_loop(1, NW, send_u, 0, unroll=3)
+        each_wide(send_u)
 
         def keep_u(size, x0=x0, p=p):
             c = pltpu.make_async_copy(
@@ -534,7 +538,7 @@
             jnp.concatenate(
                 [
                     ub[pl.ds(128 * x0 + k * p + x, 64, stride=2 * p), :]
-                    for x0, p in CHUNKS
+                    for x0, p in sorted(CHUNKS)
                     for x in range(p)
                 ],
                 axis=0,
@@ -558,13 +562,11 @@
         def back(size, i=i, x0=x0, p=p):
             here = pl.ds(100 * x0 + tile * p, size)
 
-            def send_v(d, carry):
-                v = lax.rem(me + d, NW)
-                src = vb.at[pl.ds(128 * x0 + v * 2 * p, size)]
-                send(src, s2.at[here], vs.at[i], vr.at[i], {"wide": device_of(v)})
-                return carry
-
-            lax.fori_loop(1, NW, send_v, 0, unroll=3)
+            def send_v(x, c, y):
+                src = vb.at[pl.ds(128 * x0 + (x * 16 + c * 8 + y) * 2 * p, size)]
+                send(src, s2.at[here], vs.at[i], vr.at[i], device(x, c, y))
+
+            each_wide(send_v)
             c = pltpu.make_async_copy(
                 vb.at[pl.ds(128 * x0 + me * 2 * p, size)], s2.at[here], lsem.at[5]
             )
@@ -610,7 +612,7 @@
                 pack_plane(n2s[i], m, lines[r : r + CY, cols])
         own = pltpu.make_async_copy(n2s[i].at[n], n2r[i].at[n], lsem.at[7])
         own.start()
-        for d in range(1, NN):
+        for d in FAR:
             v = lax.rem(n + d, NN)
             send(n2s[i].at[v], n2r[i].at[n], n2ss.at[i], n2rs.at[i], {"narrow": v})
         own.wait()
@@ -631,17 +633,18 @@
         ).reshape(p, CY, NZ)
         start_halo(vp, (i, "x"))
         start_halo(vp, (i, "y"))
-        if i > 0:
-            q0, q = CHUNKS[i - 1]
-            wait_halo(vp, (i - 1, "y"))
-            along_y(vp, my, ky, 3 + q0, 3 + q0 + q)
-    last = len(CHUNKS) - 1
-    wait_halo(vp, (last, "y"))
-    along_y(vp, my, ky, 3 + CHUNKS[last][0], 3 + CX)
-    wait_halo(vp, (last, "x"))
+        if i == 1:
+            wait_halo(vp, (0, "y"))
+            along_y(vp, my, ky, 3, 6)
+
+    wait_halo(vp, (1, "y"))
+    along_y(vp, my, ky, 9, 13)
+    wait_halo(vp, (0, "x"))
+    along_y(vp, my, ky, 13, 16)
+    wait_halo(vp, (1, "x"))
     along_y(vp, my, ky, 0, 3)
-    wait_halo(vp, (0, "x"))
-    along_y(vp, my, ky, CX + 3, CX + 6)
+    wait_halo(vp, (2, "y"))
+    along_y(vp, my, ky, 6, 9)
     along_xz(my, ky, first, second, bands, fresh)
 
     precond = vp[3:13, 8:48, :].reshape(CX * CY, NZ)
@@ -659,18 +662,17 @@
         row = jnp.where(lane == i, item, row)
     red[0] = row
     rb1[n] = row
-    for d in range(1, NN):
+    for d in FAR:
         send(red.at[0], rb1.at[n], rs1, rr1, {"narrow": lax.rem(n + d, NN)})
     done(rb1.at[pl.ds(0, 7)], rr1)
     row = jnp.sum(rb1[...], axis=0)
     red[1] = row
     rb2[w] = row
 
-    def send_r(d, carry):
-        send(red.at[1], rb2.at[w], rs2, rr2, {"wide": lax.rem(w + d, NW)})
-        return carry
-
-    lax.fori_loop(1, NW, send_r, 0)
+    def send_r(x, c, y):
+        send(red.at[1], rb2.at[w], rs2, rr2, device(x, c, y))
+
+    each_wide(send_r)
     done(rb2.at[pl.ds(0, 63)], rr2)
     row = jnp.sum(rb2[...], axis=0)
     now, self_term, cross, curvature = (

time: 105 us -> 99.1 us (0.944)
  Pallas kernels: 104 us -> 97.6 us
    pallas_call x1, Pallas kernels: 103 us -> 96.3 us  [per_device(): pl.pallas_call(kernel, out_shape=(brick, brick, brick), in_specs=[pl.Bloc...]
where the time goes in v6:
time: 99.1 us; the launch traced here: 98.9 us
  Pallas kernels  97.6 us (98%)
  between operations  1.29 us (1%)
    pallas_call x1, Pallas kernels, per_device(): pl.pallas_call(kernel, out_shape=(brick, brick, brick), in_specs=[pl.Bloc...  96.3 us

profile of v6, /device:TPU:1, one launch (start us, length us, event | category | flops | bytes accessed | tf_op | source)
XLA Modules:
  0.0 98.9 jit_solution(18342721841213491464)
XLA Ops:
  1.3 96.3 %iterate.1 = (f32[10,40,320]{2,1,0:T(8,128)S(1)}, f32[10,40,320]{2,1,0:T(8,128)S(1)}, f32[10,40,320]{2,1,0:T(8,128)S(1)}) custom-call(f32[1]{0:T(128)S(6)} %copy.13.prev_ref, f32[640]{0:T(1024)} %ex_hbm.1, f32[320]{0:T(512)} %ey_hbm.1, f32[320]{0:T(512)} %ez_hbm.1, f32[10,40,320]{2,1,0:T(8,128)} %sol_ref.1, f32[10,40,320]{2,1,0:T(8,128)} %res_ref.1, ...), custom_call_target="tpu_custom_call" | custom-call | tf_op jit(solution)/shard_map/iterate/pallas_call | solution.py:783
  97.6 1.3 %finish.1 = (f32[10,40,320]{2,1,0:T(8,128)}, f32[10,40,320]{2,1,0:T(8,128)}, f32[10,40,320]{2,1,0:T(8,128)}) custom-call(f32[10,40,320]{2,1,0:T(8,128)S(1)} %get-tuple-element.6.sol, f32[10,40,320]{2,1,0:T(8,128)S(1)} %get-tuple-element.7.res, f32[10,40,320]{2,1,0:T(8,128)S(1)} %get-tuple-element.8.direction), custom_call_target="tpu_custom_call" | custom-call | tf_op jit(solution)/shard_map/finish/pallas_call | solution.py:800

commit v7 on v6

--- a/solution.py
+++ b/solution.py
@@ -39,6 +39,15 @@
         )
 
     return one(a[0], b[0]) + one(a[0], b[1]) + one(a[1], b[0])
+
+
+def ends(x):
+    high, low = split(x)
+    return jnp.concatenate([high, low, high], axis=0)
+
+
+def long_dot(a, b):
+    return lax.dot_general(a, b, (((1,), (0,)), ((), ())), preferred_element_type=jnp.float32)
 
 
 def keep(ref, x):
@@ -103,6 +112,22 @@
     f = split(second[...].reshape(CX * CY, NZ))
     m, k = ((bands[i, 0], bands[i, 1]) for i in range(2))
     out[...] = dot3(g, m, 1, 0) + dot3(f, k, 1, 0)
+
+
+def pack_basis(dst, src):
+    dst[0:40, :] = src[:, 0:128]
+    dst[40:80, :] = src[:, 128:256]
+    dst[80:104, 0:64] = src[0:24, 256:320]
+    dst[80:96, 64:128] = src[24:40, 256:320]
+
+
+def unpack_basis(dst, src):
+    for m in range(NN):
+        r = m * CY
+        dst[r : r + CY, 0:128] = src[m, 0:40, :]
+        dst[r : r + CY, 128:256] = src[m, 40:80, :]
+        dst[r : r + 24, 256:320] = src[m, 80:104, 0:64]
+        dst[r + 24 : r + CY, 256:320] = src[m, 80:96, 64:128]
 
 
 def pack_plane(dst, m, rows):
@@ -147,6 +172,13 @@
     n1r,
     wxp,
     wide4,
+    zraw,
+    yraw,
+    bzp,
+    byp,
+    wzp,
+    wyp,
+    part,
     wxr,
     wxc,
     wyr,
@@ -220,23 +252,19 @@
 
     get_res = pltpu.make_async_copy(res_ref, res, lsem.at[8])
     get_dir = pltpu.make_async_copy(dir_ref, vd.at[pl.ds(3, CX), pl.ds(8, CY)], lsem.at[9])
-    get_sol = pltpu.make_async_copy(sol_ref, sol, lsem.at[10])
+    get_sol = pltpu.make_async_copy(sol_ref, sol, lsem.at[6])
     small = [
         pltpu.make_async_copy(a, b, lsem.at[11 + i])
         for i, (a, b) in enumerate(
             ((ex_hbm, ex_ref), (ey_hbm, ey_ref), (ez_hbm, ez_ref))
         )
     ]
-    for c in [get_res, get_dir, *small, get_sol]:
+    bases = [
+        pltpu.make_async_copy(bz_ref, zraw, lsem.at[0]),
+        pltpu.make_async_copy(by_ref, yraw, lsem.at[1]),
+    ]
+    for c in [*bases, get_res, get_dir, *small, get_sol]:
         c.start()
-
-    for v in (vd, vp):
-        for p in (0, 1, 2, 13, 14, 15):
-            v[p] = jnp.zeros((56, NZ), jnp.float32)
-        for p in range(3, 13):
-            v[p, 0:8, :] = jnp.zeros((8, NZ), jnp.float32)
-            v[p, 48:56, :] = jnp.zeros((8, NZ), jnp.float32)
-    ub[...] = jnp.zeros_like(ub)
 
     def greet(x, c, y):
         pl.semaphore_signal(barrier, inc=1, device_id=device(x, c, y), device_id_type=MESH)
@@ -252,11 +280,10 @@
                 barrier, inc=1, device_id={"wide": a, "narrow": b}, device_id_type=MESH
             )
 
-    keep(bands.at[0], band(MASS))
-    keep(bands.at[1], band(STIFF))
-    for c in small:
+    for c in bases:
         c.wait()
-    exc[...] = jnp.transpose(jnp.broadcast_to(ex_ref[...].reshape(1, NX), (128, NX)))
+    pack_basis(bzp, zraw)
+    pack_basis(byp, yraw)
 
     pl.semaphore_wait(barrier, NW - 1 + NN - 1 + 4)
 
@@ -277,37 +304,34 @@
     def near(d):
         return core == (d + 1) % 2
 
-    def rows_of(v):
-        return pl.ds(pl.multiple_of(v * CY, 8), CY)
-
     def share(own, whole, ssem, rsem):
         for d in FAR:
 
             @pl.when(near(d))
             def _(d=d):
                 at = {"narrow": lax.rem(n + d, NN)}
-                send(own, whole.at[rows_of(n)], ssem, rsem.at[d], at)
+                send(own, whole.at[n], ssem, rsem.at[d], at)
 
     def hand_over(whole, rsem, fsem, gsem):
         for d in FAR:
 
             @pl.when(near(d))
             def _(d=d):
-                m = rows_of(lax.rem(n + NN - d, NN))
+                m = lax.rem(n + NN - d, NN)
                 done(whole.at[m], rsem.at[d])
                 send(whole.at[m], whole.at[m], fsem, gsem, {"wide": sibling})
 
-    def by_core(whole, sem, first_rows):
+    def by_core(whole, sem, blocks):
         @pl.when(core == 0)
         def _():
-            done(whole.at[pl.ds(0, first_rows)], sem)
+            done(whole.at[pl.ds(0, blocks)], sem)
 
         @pl.when(core == 1)
         def _():
-            done(whole.at[pl.ds(0, 280 - first_rows)], sem)
-
-    ownz = pltpu.make_async_copy(bz_ref, wz.at[rows_of(n)], lsem.at[0])
-    owny = pltpu.make_async_copy(by_ref, wy.at[rows_of(n)], lsem.at[1])
+            done(whole.at[pl.ds(0, 7 - blocks)], sem)
+
+    ownz = pltpu.make_async_copy(bzp, wzp.at[n], lsem.at[14])
+    owny = pltpu.make_async_copy(byp, wyp.at[n], lsem.at[10])
     rows_x = pl.ds(gy * CX, CX)
     for k in range(5):
         pltpu.make_async_copy(
@@ -315,8 +339,8 @@
         ).start()
     ownz.start()
     owny.start()
-    share(bz_ref, wz, zbs, zbr)
-    share(by_ref, wy, ybs, ybr)
+    share(bzp, wzp, zbs, zbr)
+    share(byp, wyp, ybs, ybr)
 
     done(wx.at[:, gx, core, rows_x], lsem.at[2])
     for d in FAR:
@@ -403,7 +427,25 @@
             def _(key=key, item=item, j=j, a=a, b=b, planes=planes):
                 done(v.at[side_of(a, planes, 0), rows[b][0]], hs.at[slot(key, item, j)])
 
-    hand_over(wz, zbr, zfs, zfr)
+    keep(bands.at[0], band(MASS))
+    keep(bands.at[1], band(STIFF))
+    for c in small:
+        c.wait()
+    exc[...] = jnp.transpose(jnp.broadcast_to(ex_ref[...].reshape(1, NX), (128, NX)))
+    fills = (
+        (w == 0, slice(0, 3), slice(0, 56)),
+        (w == NW - 1, slice(13, 16), slice(0, 56)),
+        (n == 0, slice(0, 16), slice(0, 8)),
+        (n == NN - 1, slice(0, 16), slice(48, 56)),
+    )
+    for edge, ps, rs in fills:
+
+        @pl.when(edge)
+        def _(ps=ps, rs=rs):
+            for v in (vd, vp):
+                v[ps, rs, :] = jnp.zeros((ps.stop - ps.start, rs.stop - rs.start, NZ), jnp.float32)
+
+    hand_over(wzp, zbr, zfs, zfr)
     done(wx.at[:, 0, 0, pl.ds(0, 70)], xr.at[0])
     for e in (2, 1, 3):
         at = {"wide": lax.rem(gx + e, 4) * 16 + gy * 2 + core}
@@ -411,7 +453,8 @@
 
     get_res.wait()
     ownz.wait()
-    by_core(wz, zfr, 120)
+    by_core(wzp, zfr, 3)
+    unpack_basis(wz, wzp)
     for i, (x0, p) in enumerate(CHUNKS):
         flat = dot(wz[...], res[x0 : x0 + p].reshape(p * CY, NZ), 0, 1)
         n1s[i][:, 0:40, :] = flat[:, 0:120].reshape(NN, CY, 120)
@@ -424,7 +467,7 @@
             at = {"narrow": v}
             send(n1s[i].at[v], n1r[i].at[n], n1ss.at[i], n1rs.at[i, n], at)
 
-    hand_over(wy, ybr, yfs, yfr)
+    hand_over(wyp, ybr, yfs, yfr)
     get_dir.wait()
     start_halo(vd, "old")
     tile = first_tile(gx, core, gy)
@@ -432,7 +475,8 @@
     one = jnp.logical_not(two)
 
     owny.wait()
-    by_core(wy, yfr, 120)
+    by_core(wyp, yfr, 3)
+    unpack_basis(wy, wyp)
     keep(wyr, wy[...])
 
     for i, (x0, p) in enumerate(CHUNKS):
@@ -519,10 +563,18 @@
                     k, g // 2, g % 2, pl.ds(x, 8, stride=CX), :
                 ]
         cols = slice(128 * k, 128 * k + 128)
-        wxr[0, :, cols], wxr[1, :, cols] = split(wxp[k])
-        wxc[0, cols, :], wxc[1, cols, :] = split(jnp.transpose(wxp[k]))
+        high, low = split(wxp[k])
+        wxr[:, 128 * k : 128 * k + 128] = high
+        wxr[:, NX + 128 * k : NX + 128 * k + 128] = high
+        wxr[:, 2 * NX + 128 * k : 2 * NX + 128 * k + 128] = low
+        for i, (x0, p) in enumerate(CHUNKS):
+            high, low = split(jnp.transpose(wxp[k, 64 * x0 : 64 * (x0 + p), :]))
+            wxc[i][cols, 0 : 64 * p] = high
+            wxc[i][cols, 64 * p : 128 * p] = high
+            wxc[i][cols, 128 * p : 192 * p] = low
     keep(wyc, jnp.transpose(wy[...]))
     keep(wzc, jnp.transpose(wz[...]))
+    spectral = None
     for i, (x0, p) in enumerate(CHUNKS):
 
         @pl.when(two)
@@ -530,29 +582,38 @@
             done(ub.at[pl.ds(0, 126 * p)], ur.at[i])
 
         @pl.when(one)
-        def _(i=i, p=p):
+        def _(i=i, x0=x0, p=p):
+            for x in range(p):
+                ub[pl.ds(128 * x0 + p + x, 64, stride=2 * p), :] = jnp.zeros((64, 128), jnp.float32)
             done(ub.at[pl.ds(0, 63 * p)], ur.at[i])
 
-    both = jnp.concatenate(
-        [
-            jnp.concatenate(
-                [
-                    ub[pl.ds(128 * x0 + k * p + x, 64, stride=2 * p), :]
-                    for x0, p in sorted(CHUNKS)
-                    for x in range(p)
-                ],
-                axis=0,
-            )
-            for k in range(2)
-        ],
-        axis=1,
-    )
-    spectral = dot3((wxc[0], wxc[1]), split(both), 1, 0)
+        if i == len(CHUNKS) - 1:
+            pass
+        both = jnp.concatenate(
+            [
+                jnp.concatenate(
+                    [
+                        ub[pl.ds(128 * x0 + k * p + x, 64, stride=2 * p), :]
+                        for x in range(p)
+                    ],
+                    axis=0,
+                )
+                for k in range(2)
+            ],
+            axis=1,
+        )
+        term = long_dot(wxc[i][...], ends(both))
+        if i == 0:
+            part[...] = term
+        elif i == 1:
+            part[...] += term
+        else:
+            spectral = part[...] + term
     cols = jnp.concatenate([exc[...], exc[...]], axis=1)
-    spectral = split(spectral / (cols + shift))
+    spectral = ends(spectral / (cols + shift))
     for i, (x0, p) in enumerate(CHUNKS):
         span = slice(64 * x0, 64 * (x0 + p))
-        inverse = dot3((wxr[0, span, :], wxr[1, span, :]), spectral, 1, 0)
+        inverse = long_dot(wxr[span, :], spectral)
         for x in range(p):
             for k in range(2):
                 vb[pl.ds(128 * x0 + k * p + x, 64, stride=2 * p), :] = inverse[
@@ -643,6 +704,13 @@
     along_y(vp, my, ky, 13, 16)
     wait_halo(vp, (1, "x"))
     along_y(vp, my, ky, 0, 3)
+    precond = vp[3:13, 8:48, :].reshape(CX * CY, NZ)
+    direction = vd[3:13, 8:48, :].reshape(CX * CY, NZ)
+    early = (
+        total(res[...].reshape(CX * CY, NZ), precond),
+        total(precond, image[...]),
+        total(direction, image[...]),
+    )
     wait_halo(vp, (2, "y"))
     along_y(vp, my, ky, 6, 9)
     along_xz(my, ky, first, second, bands, fresh)
@@ -650,12 +718,7 @@
     precond = vp[3:13, 8:48, :].reshape(CX * CY, NZ)
     direction = vd[3:13, 8:48, :].reshape(CX * CY, NZ)
     res2 = res[...].reshape(CX * CY, NZ)
-    items = (
-        total(res2, precond),
-        total(precond, fresh[...]),
-        total(precond, image[...]),
-        total(direction, image[...]),
-    )
+    items = (early[0], total(precond, fresh[...]), early[1], early[2])
     lane = lax.broadcasted_iota(jnp.int32, (1, 128), 1)
     row = jnp.zeros((1, 128), jnp.float32)
     for i, item in enumerate(items):
@@ -689,10 +752,10 @@
     res_out[...] = (res2 - alpha * new_image).reshape(CX, CY, NZ)
     dir_out[...] = direction.reshape(CX, CY, NZ)
 
-    by_core(wz, zbs, 160)
-    by_core(wz, zfs, 160)
-    by_core(wy, ybs, 160)
-    by_core(wy, yfs, 160)
+    by_core(wzp, zbs, 4)
+    by_core(wzp, zfs, 4)
+    by_core(wyp, ybs, 4)
+    by_core(wyp, yfs, 4)
     done(wx.at[:, 0, 0, pl.ds(0, 70)], xs.at[0])
     done(wx.at[:, pl.ds(0, 3), 0], xs.at[1])
     done(wx.at[:, :, 0], xs.at[2])
@@ -718,10 +781,13 @@
     done(rb2.at[pl.ds(0, 63)], rs2)
 
 
-def finish(sol, res, direction, sol_out, res_out, dir_out):
-    sol_out[...] = sol[...]
-    res_out[...] = res[...]
-    dir_out[...] = direction[...]
+def finish(sol, res, direction, sol_out, res_out, dir_out, sems):
+    pairs = ((sol, sol_out), (res, res_out), (direction, dir_out))
+    copies = [pltpu.make_async_copy(a, b, sems.at[i]) for i, (a, b) in enumerate(pairs)]
+    for c in copies:
+        c.start()
+    for c in copies:
+        c.wait()
 
 
 def per_device(sol, res, direction, prev, bx, by, bz, ex, ey, ez):
@@ -750,8 +816,15 @@
         tuple((NN, r, 120) for r in ROWS),
         (5, NX, 128),
         (NZ, 160),
-        [2, NX, NX],
-        [2, NX, NX],
+        (CY, NZ),
+        (CY, NZ),
+        (104, 128),
+        (104, 128),
+        (NN, 104, 128),
+        (NN, 104, 128),
+        (NX, 256),
+        [NX, 3 * NX],
+        tuple([NX, 192 * p] for _, p in CHUNKS),
         [2, NZ, NZ],
         [2, NZ, NZ],
         [2, NZ, NZ],
@@ -772,8 +845,8 @@
     sems += [(2, 12), (2, 12), (k,), (k, 8)] + [(k,)] * 6 + [()] * 4
 
     def space(s):
-        if isinstance(s[0], tuple):
-            return [pltpu.VMEM(t, f32) for t in s]
+        if isinstance(s[0], (tuple, list)):
+            return [space(t) for t in s]
         return pltpu.VMEM(tuple(s), jnp.bfloat16 if isinstance(s, list) else f32)
 
     far = [
@@ -801,7 +874,8 @@
         finish,
         out_shape=(brick, brick, brick),
         in_specs=[vmem] * 3,
-        out_specs=(vmem, vmem, vmem),
+        out_specs=(hbm, hbm, hbm),
+        scratch_shapes=[dma((3,))],
         compiler_params=pltpu.CompilerParams(vmem_limit_bytes=12 << 20),
         name="finish",
     )(*outs)

time: 99.1 us -> 97.2 us (0.981)
  Pallas kernels: 97.6 us -> 95.6 us
    pallas_call x1, Pallas kernels: 96.3 us -> 94.3 us  [per_device(): pl.pallas_call(kernel, out_shape=(brick, brick, brick), in_specs=[pl.Bloc...]
where the time goes in v7:
time: 97.2 us; the launch traced here: 97 us
  Pallas kernels  95.6 us (98%)
  between operations  1.45 us (1%)
    pallas_call x1, Pallas kernels, per_device(): pl.pallas_call(kernel, out_shape=(brick, brick, brick), in_specs=[pl.Bloc...  94.3 us

profile of v7, /device:TPU:1, one launch (start us, length us, event | category | flops | bytes accessed | tf_op | source)
XLA Modules:
  0.0 97.0 jit_solution(5307924304323008247)
XLA Ops:
  1.3 94.3 %iterate.1 = (f32[10,40,320]{2,1,0:T(8,128)S(1)}, f32[10,40,320]{2,1,0:T(8,128)S(1)}, f32[10,40,320]{2,1,0:T(8,128)S(1)}) custom-call(f32[1]{0:T(128)S(6)} %copy.13.prev_ref, f32[640]{0:T(1024)} %ex_hbm.1, f32[320]{0:T(512)} %ey_hbm.1, f32[320]{0:T(512)} %ez_hbm.1, f32[10,40,320]{2,1,0:T(8,128)} %sol_ref.1, f32[10,40,320]{2,1,0:T(8,128)} %res_ref.1, ...), custom_call_target="tpu_custom_call" | custom-call | tf_op jit(solution)/shard_map/iterate/pallas_call | solution.py:856
  95.6 1.3 %finish.1 = (f32[10,40,320]{2,1,0:T(8,128)}, f32[10,40,320]{2,1,0:T(8,128)}, f32[10,40,320]{2,1,0:T(8,128)}) custom-call(f32[10,40,320]{2,1,0:T(8,128)S(1)} %get-tuple-element.6.sol, f32[10,40,320]{2,1,0:T(8,128)S(1)} %get-tuple-element.7.res, f32[10,40,320]{2,1,0:T(8,128)S(1)} %get-tuple-element.8.direction), custom_call_target="tpu_custom_call" | custom-call | tf_op jit(solution)/shard_map/finish/pallas_call | solution.py:873

commit v8 on v7

--- a/solution.py
+++ b/solution.py
@@ -830,10 +830,10 @@
         [2, NZ, NZ],
         (400, NZ),
         (400, NZ),
-        (1000, 128),
-        (2 * NX, 128),
-        (2 * NX, 128),
-        (1000, 128),
+        (1040, 128),
+        (2 * NX + 16, 128),
+        (2 * NX + 16, 128),
+        (1040, 128),
         tuple((NN, r, 120) for r in ROWS),
         tuple((NN, r, 120) for r in ROWS),
         (2, 1, 128),

time: 97.2 us -> 97.2 us (level)
  no operation moved by 1% of the time
where the time goes in v8:
time: 97.2 us; the launch traced here: 97 us
  Pallas kernels  95.6 us (98%)
  between operations  1.45 us (1%)
    pallas_call x1, Pallas kernels, per_device(): pl.pallas_call(kernel, out_shape=(brick, brick, brick), in_specs=[pl.Bloc...  94.3 us

profile of v8, /device:TPU:1, one launch (start us, length us, event | category | flops | bytes accessed | tf_op | source)
XLA Modules:
  0.0 97.0 jit_solution(11555672829440120015)
XLA Ops:
  1.3 94.3 %iterate.1 = (f32[10,40,320]{2,1,0:T(8,128)S(1)}, f32[10,40,320]{2,1,0:T(8,128)S(1)}, f32[10,40,320]{2,1,0:T(8,128)S(1)}) custom-call(f32[1]{0:T(128)S(6)} %copy.13.prev_ref, f32[640]{0:T(1024)} %ex_hbm.1, f32[320]{0:T(512)} %ey_hbm.1, f32[320]{0:T(512)} %ez_hbm.1, f32[10,40,320]{2,1,0:T(8,128)} %sol_ref.1, f32[10,40,320]{2,1,0:T(8,128)} %res_ref.1, ...), custom_call_target="tpu_custom_call" | custom-call | tf_op jit(solution)/shard_map/iterate/pallas_call | solution.py:856
  95.6 1.3 %finish.1 = (f32[10,40,320]{2,1,0:T(8,128)}, f32[10,40,320]{2,1,0:T(8,128)}, f32[10,40,320]{2,1,0:T(8,128)}) custom-call(f32[10,40,320]{2,1,0:T(8,128)S(1)} %get-tuple-element.6.sol, f32[10,40,320]{2,1,0:T(8,128)S(1)} %get-tuple-element.7.res, f32[10,40,320]{2,1,0:T(8,128)S(1)} %get-tuple-element.8.direction), custom_call_target="tpu_custom_call" | custom-call | tf_op jit(solution)/shard_map/finish/pallas_call | solution.py:873
